TPU v7x, 256 devices: a whole 4x4x8 slice. The times are simulated.
256 devices in a mesh: view: 8 (over x, core), slab: 32 (over y, z).
Axes of the slice: x: 4, y: 4, z: 8, core: 2. Of those that a mesh axis runs over, the one named last changes fastest.
Arguments:
- image: float32 [128, 512, 512], P('slab'), may hold values from 0.1 to 10
- sensitivity: float32 [128, 512, 512], P('slab', 'view'), may hold values from 0.5 to 4
- resample_x: bfloat16 [16, 512, 512], P('view'), may hold values from 0 to 1, as said below
- resample_y: bfloat16 [16, 512, 512], P('view'), may hold values from 0 to 1, as said below
- tof_kernel: bfloat16 [16, 16, 512], P('view'), may hold values from 0.00019454956 to 0.0078125
- axial_mix: float32 [16, 128, 128], P('view'), may hold values from 0 to 1
- background: float32 [16, 16, 512, 128], P('view', None, 'slab'), may hold values from 0.5 to 2
- counts: int32 [16, 16, 512, 128], P('view', None, 'slab'), may hold values from 0 to 19
Outputs:
- new_image: float32 [128, 512, 512], P('slab', 'view')
Inputs may be any that keep to these rules, and one draw needn't show every extreme that they name: resample_x[v, a, x] is zero where |x - a| > 3. resample_y[v, y, b] is zero where |b - y| > 3.
All inputs are finite; a program needn't handle non-finite values.
Results may differ from a plain program's by a relative error of at most 0.00052.
Values may be sent and summed in bfloat16 or wider, within the bound.
A program may use at most 64 MiB of HBM per device.

v0:
```python
import jax
import jax.numpy as jnp
from jax import lax
from jax.sharding import PartitionSpec as P


def local(image, sensitivity, resample_x, resample_y, tof_kernel, axial_mix, background, counts):
    highest = lax.Precision.HIGHEST
    image_low = image.astype(jnp.bfloat16)
    along_y = jnp.einsum(
        "zxy,vyb->vzxb", image_low, resample_y, preferred_element_type=jnp.float32
    ).astype(jnp.bfloat16)
    rotated = jnp.einsum(
        "vzxb,vax->vzba", along_y, resample_x, preferred_element_type=jnp.float32
    ).astype(jnp.bfloat16)
    gathered = lax.all_to_all(rotated, "slab", split_axis=2, concat_axis=1, tiled=True)
    integrals = jnp.einsum(
        "vka,vzba->vkbz", tof_kernel, gathered, preferred_element_type=jnp.float32
    )
    expected = background + jnp.einsum("vkbz,vcz->vkbc", integrals, axial_mix, precision=highest)
    ratios = counts.astype(jnp.float32) / expected
    back_mixed = jnp.einsum("vkbc,vcz->vkbz", ratios, axial_mix, precision=highest).astype(
        jnp.bfloat16
    )
    spread = jnp.einsum(
        "vka,vkbz->vzba", tof_kernel, back_mixed, preferred_element_type=jnp.float32
    ).astype(jnp.bfloat16)
    frames = lax.all_to_all(spread, "slab", split_axis=1, concat_axis=2, tiled=True)
    unrotated = jnp.einsum(
        "vzba,vyb->vzya", frames, resample_y, preferred_element_type=jnp.float32
    ).astype(jnp.bfloat16)
    own_rows = image.shape[1] // lax.axis_size("view")
    gradient = lax.psum_scatter(
        jnp.einsum("vzya,vax->xzy", unrotated, resample_x, preferred_element_type=jnp.float32),
        "view",
        scatter_dimension=0,
        tiled=True,
    )
    gradient = jnp.transpose(gradient, (1, 0, 2))
    current = lax.dynamic_slice_in_dim(image, lax.axis_index("view") * own_rows, own_rows, 1)
    return current * gradient / sensitivity


def solution(mesh):
    in_specs = (
        P("slab", None, None),
        P("slab", "view", None),
        P("view", None, None),
        P("view", None, None),
        P("view", None, None),
        P("view", None, None),
        P("view", None, "slab", None),
        P("view", None, "slab", None),
    )
    out_specs = P("slab", "view", None)
    return jax.shard_map(local, mesh=mesh, in_specs=in_specs, out_specs=out_specs, check_vma=False)
```

profile of v0, /device:TPU:1, one launch (start us, length us, event | category | flops | bytes accessed | tf_op | source)
XLA Modules:
  0.0 340.1 jit_solution(16715669214694171133)
XLA Ops:
  6.5 0.0 copy-start
  6.5 0.0 all-reduce.3.cloned.1.call-start
  6.5 1.2 copy-done
  7.8 8.0 %fusion.8 = bf16[2,4,512,512]{3,2,1,0:T(8,128)(2,1)} fusion(f32[4,512,512]{2,1,0:T(8,128)} %param.8, bf16[2,512,512]{2,1,0:T(8,128)(2,1)S(1)} %copy-done, bf16[2,512,512]{2,1,0:T(8,128)(2,1)} %param.10), kind=kOutput, calls=%fused_computation.9 | convolution fusion | flops 4300210176 | bytes 10485760 | tf_op jit(solution)/shard_map/vzxb,vax->vzba/dot_general | solution.py:13
  15.7 5.4 %copy.44 = bf16[2,4,512,512]{3,1,0,2:T(4,128)(2,1)S(1)} copy(bf16[2,4,512,512]{3,2,1,0:T(8,128)(2,1)} %fusion.8) | data formatting | bytes 8388608 | tf_op jit(solution)/shard_map/convert_element_type | solution.py:15
  21.1 103.9 %all_to_all.36 = bf16[2,4,512,512]{3,1,0,2:T(4,128)(2,1)S(1)} all-to-all(bf16[2,4,512,512]{3,1,0,2:T(4,128)(2,1)S(1)} %copy.44), channel_id=1, replica_groups=mesh['view'=8,'slab'=32] {'slab'}, dimensions={2} | all-to-all | bytes 8388608 | tf_op jit(solution)/shard_map/all_to_all | solution.py:16
  125.0 1.4 copy.45
  126.4 0.0 copy-start.3
  126.4 0.6 copy.46
  127.1 0.1 copy-done.3
  127.2 0.0 copy-start.2
  127.2 1.2 convolution_bitcast_fusion
  128.4 0.8 copy.47
  129.3 0.0 copy-done.2
  129.3 1.4 fusion.24
  130.7 0.4 convolution_convert_fusion
  131.2 2.0 convert_bitcast_fusion
  133.2 2.4 copy.49
  135.6 100.6 %all_to_all.37 = bf16[2,128,16,512]{3,2,0,1:T(8,128)(2,1)S(1)} all-to-all(bf16[2,128,16,512]{3,2,0,1:T(8,128)(2,1)S(1)} %copy.49), channel_id=1, replica_groups=mesh['view'=8,'slab'=32] {'slab'}, dimensions={1} | all-to-all | bytes 8388608 | tf_op jit(solution)/shard_map/all_to_all | solution.py:28
  236.2 0.0 copy-start.4
  236.2 2.4 copy.51
  238.6 0.0 copy-done.4
  238.6 9.2 %fusion.13 = f32[512,4,512]{0,2,1:T(8,128)} fusion(bf16[2,4,512,512]{3,2,1,0:T(8,128)(2,1)} %bitcast.73, bf16[2,512,512]{2,1,0:T(8,128)(2,1)S(1)} %copy-done.4, bf16[2,512,512]{2,1,0:T(8,128)(2,1)S(1)} %copy-done), kind=kOutput, calls=%fused_computation.11 | convolution fusion | flops 4297064448 | bytes 10485760 | tf_op jit(solution)/shard_map/vzya,vax->xzy/dot_general | solution.py:34
  247.8 5.5 %copy.54 = f32[512,4,512]{2,1,0:T(4,128)} copy(f32[512,4,512]{0,2,1:T(8,128)} %fusion.13) | data formatting | bytes 8388608 | tf_op jit(solution)/shard_map/vzya,vax->xzy/dot_general | solution.py:34
  253.3 0.0 copy-start.5
  253.3 0.0 copy-start.1
  253.3 0.0 all-reduce.3.cloned.1.call-update
  253.3 0.6 copy-done.5
  254.0 0.6 dynamic-slice
  255.2 74.8 %all-reduce.3.cloned.1.call-done = f32[512,4,512]{2,1,0:T(4,128)} async-done(((f32[512,4,512]{2,1,0:T(4,128)}), f32[512,4,512]{2,1,0:T(4,128)}) %all-reduce.3.cloned.1.call-update) | async-done | bytes 4194320
  330.0 1.1 constant_dynamic-slice_fusion
  331.1 0.0 copy-done.1
  331.1 2.1 fusion.31
Async XLA Ops:
  6.5 1.2 copy-start
  6.5 323.5 %all-reduce.3.cloned.1.call-start = ((), (), s32[]{:S(2)}) async-start(), calls=%async_computation.2 | async-start | bytes 8388608
  126.4 0.8 copy-start.3
  127.2 2.1 copy-start.2
  236.2 2.5 copy-start.4
  253.3 0.7 copy-start.5
  253.3 77.8 %copy-start.1 = (f32[4,64,512]{2,1,0:T(8,128)S(1)}, f32[4,64,512]{2,1,0:T(8,128)}, u32[]{:S(2)}) copy-start(f32[4,64,512]{2,1,0:T(8,128)} %param.9) | copy-start | bytes 1572868
Sparse Core Ops, SparseCore 0:
  253.4 76.5 all-reduce.2
where the time goes:
time: 341 us; the launch traced here: 340 us
  blocking collectives  204 us (60%)
  waiting for transfers between devices  74.9 us (22%)
  local copies, waits for them, and re-layouts  22.3 us (7%)
  matrix products  22.3 us (7%)
  between operations  14.1 us (4%)
    all_to_all x1, blocking collectives, local(): lax.all_to_all(rotated, 'slab', split_axis=2, concat_axis=1, tiled=True)  104 us
    all_to_all x1, blocking collectives, local(): lax.all_to_all(spread, 'slab', split_axis=1, concat_axis=2, tiled=True)  101 us
    unnamed x2, waiting for transfers between devices  74.9 us
    dot_general x1, matrix products, local(): jnp.einsum('vzya,vax->xzy', unrotated, resample_x, preferred_element_type...  9.19 us
    dot_general x1, matrix products, local(): jnp.einsum('vzxb,vax->vzba', along_y, resample_x, preferred_element_type=...  7.96 us
  transfers between devices with their start and end apart: 1, of which 1 were waited for; matrix products, arithmetic and copies ran while one was open for 0% of the time, Pallas kernels for 0%

commit v1 on v0

--- a/solution.py
+++ b/solution.py
@@ -13,19 +13,28 @@
     rotated = jnp.einsum(
         "vzxb,vax->vzba", along_y, resample_x, preferred_element_type=jnp.float32
     ).astype(jnp.bfloat16)
-    gathered = lax.all_to_all(rotated, "slab", split_axis=2, concat_axis=1, tiled=True)
+    views, own, bins, _ = rotated.shape
+    tof = tof_kernel.shape[1]
     integrals = jnp.einsum(
-        "vka,vzba->vkbz", tof_kernel, gathered, preferred_element_type=jnp.float32
+        "vka,vzba->bvzk", tof_kernel, rotated, preferred_element_type=jnp.float32
     )
-    expected = background + jnp.einsum("vkbz,vcz->vkbc", integrals, axial_mix, precision=highest)
+    parts = lax.axis_size("slab")
+    gathered = lax.all_to_all(
+        integrals.reshape(parts, bins // parts, views * own * tof), "slab", split_axis=0, concat_axis=0, tiled=True
+    ).reshape(parts, bins // parts, views, own, tof)
+    gathered = jnp.transpose(gathered, (2, 4, 1, 0, 3)).reshape(views, tof, bins // parts, parts * own)
+    expected = background + jnp.einsum("vkbz,vcz->vkbc", gathered, axial_mix, precision=highest)
     ratios = counts.astype(jnp.float32) / expected
     back_mixed = jnp.einsum("vkbc,vcz->vkbz", ratios, axial_mix, precision=highest).astype(
         jnp.bfloat16
     )
-    spread = jnp.einsum(
-        "vka,vkbz->vzba", tof_kernel, back_mixed, preferred_element_type=jnp.float32
+    back_mixed = jnp.transpose(back_mixed.reshape(views, tof, bins // parts, parts, own), (3, 2, 0, 4, 1))
+    back_mixed = lax.all_to_all(
+        back_mixed.reshape(parts, bins // parts, views * own * tof), "slab", split_axis=0, concat_axis=0, tiled=True
+    ).reshape(bins, views, own, tof)
+    frames = jnp.einsum(
+        "vka,bvzk->vzba", tof_kernel, back_mixed, preferred_element_type=jnp.float32
     ).astype(jnp.bfloat16)
-    frames = lax.all_to_all(spread, "slab", split_axis=1, concat_axis=2, tiled=True)
     unrotated = jnp.einsum(
         "vzba,vyb->vzya", frames, resample_y, preferred_element_type=jnp.float32
     ).astype(jnp.bfloat16)

time: 341 us -> 174 us (0.51)
  blocking collectives: 204 us -> 36.9 us
  matrix products: 22.3 us -> 29.6 us
  local copies, waits for them, and re-layouts: 22.3 us -> 18.4 us
    all_to_all x2, blocking collectives: 204 us -> 36.9 us  [the longest x1 21.5 us: local(): lax.all_to_all(integrals.reshape(parts, bins // parts, views * own * tof)...]
    dot_general x4, matrix products: 12.7 us -> 19.8 us  [the longest x1 6.51 us: local(): jnp.einsum('zxy,vyb->vzxb', image_low, resample_y, preferred_element_type...]
    convert_element_type x2 -> x1, local copies, waits for them, and re-layouts: 7.82 us -> 0.78 us  [local(): jnp.einsum('vkbc,vcz->vkbz', ratios, axial_mix, precision=highest)]
    transpose x1 -> x2, local copies, waits for them, and re-layouts: 0.84 us -> 4.44 us  [the longest x1 2.87 us: local(): jnp.transpose(gathered, (2, 4, 1, 0, 3))]
where the time goes in v1:
time: 174 us; the launch traced here: 173 us
  waiting for transfers between devices  71.6 us (41%)
  blocking collectives  36.9 us (21%)
  matrix products  29.6 us (17%)
  local copies, waits for them, and re-layouts  18.4 us (11%)
  between operations  14.2 us (8%)
  other arithmetic  2.08 us (1%)
    unnamed x2, waiting for transfers between devices  71.6 us
    all_to_all x1, blocking collectives, local(): lax.all_to_all(integrals.reshape(parts, bins // parts, views * own * tof)...  21.5 us
    all_to_all x1, blocking collectives, local(): lax.all_to_all(back_mixed.reshape(parts, bins // parts, views * own * tof...  15.3 us
    dot_general x1, matrix products, local(): jnp.einsum('vzya,vax->xzy', unrotated, resample_x, preferred_element_type...  9.48 us
    dot_general x1, matrix products, local(): jnp.einsum('zxy,vyb->vzxb', image_low, resample_y, preferred_element_type...  6.51 us
    dot_general x1, matrix products, local(): jnp.einsum('vka,vzba->bvzk', tof_kernel, rotated, preferred_element_type=...  5.57 us
    dot_general x1, local copies, waits for them, and re-layouts, local(): jnp.einsum('vzya,vax->xzy', unrotated, resample_x, preferred_element_type...  5.47 us
    dot_general x1, matrix products, local(): jnp.einsum('vkbz,vcz->vkbc', gathered, axial_mix, precision=highest)  4.49 us
  transfers between devices with their start and end apart: 1, of which 1 were waited for; matrix products, arithmetic and copies ran while one was open for 0% of the time, Pallas kernels for 0%

profile of v1, /device:TPU:1, one launch (start us, length us, event | category | flops | bytes accessed | tf_op | source)
XLA Modules:
  0.0 172.7 jit_solution(4590930252664543603)
XLA Ops:
  6.5 0.0 copy-start
  6.5 0.0 copy-start.6
  6.5 0.0 copy-start.4
  6.5 0.0 all-reduce.3.cloned.1.call-start
  6.5 1.2 copy-done
  7.8 6.5 %fusion.17 = bf16[2,512,4,512]{3,1,2,0:T(8,128)(2,1)} fusion(f32[4,512,512]{2,1,0:T(8,128)} %param.8, bf16[2,512,512]{2,1,0:T(8,128)(2,1)S(1)} %copy-done), kind=kOutput, calls=%fused_computation.12 | convolution fusion | flops 2148532224 | bytes 9437184 | tf_op jit(solution)/shard_map/zxy,vyb->vzxb/dot_general | solution.py:10
  14.3 0.0 copy-done.6
  14.3 0.0 copy-done.4
  14.3 5.6 %fusion.32 = f32[512,2,4,16]{0,3,2,1:T(8,128)S(1)} fusion(bf16[2,512,4,512]{3,1,2,0:T(8,128)(2,1)} %fusion.17, bf16[2,512,512]{2,1,0:T(8,128)(2,1)S(1)} %copy-done.6, bf16[2,16,512]{2,1,0:T(8,128)(2,1)S(1)} %copy-done.4), kind=kOutput, calls=%fused_computation.19 | convolution fusion | flops 2216689664 | bytes 5537792 | tf_op jit(solution)/shard_map/vka,vzba->bvzk/dot_general | solution.py:18
  19.9 0.7 reshape.18
  20.6 0.0 copy-start.2
  20.6 1.3 copy.49
  21.9 21.5 %all_to_all.10 = f32[32,16,128]{2,1,0:T(8,128)S(1)} all-to-all(f32[32,16,128]{2,1,0:T(8,128)S(1)} %copy.49), channel_id=1, replica_groups=mesh['view'=8,'slab'=32] {'slab'}, dimensions={0} | all-to-all | bytes 524288 | tf_op jit(solution)/shard_map/all_to_all | solution.py:22
  43.4 0.0 copy-start.3
  43.4 1.3 copy.50
  44.7 2.9 %copy.51 = f32[2,16,16,32,4]{2,1,4,3,0:T(8,128)S(1)} copy(f32[2,16,16,32,4]{3,1,4,0,2:T(8,128)} %bitcast.76) | data formatting | bytes 524288 | tf_op jit(solution)/shard_map/transpose | solution.py:25
  47.6 0.0 copy-done.2
  47.6 0.0 copy-done.3
  47.6 4.5 %fusion.29 = f32[2,16,16,128]{3,2,1,0:T(8,128)S(1)} fusion(f32[2,16,16,128]{3,2,1,0:T(8,128)S(1)} %copy-done.3, f32[2,16,16,128]{2,1,3,0:T(8,128)S(1)} %bitcast.75, s32[2,16,16,128]{3,2,1,0:T(8,128)} %param.15, f32[2,128,128]{2,1,0:T(8,128)S(1)} %copy-done.2), kind=kOutput, calls=%fused_computation.18 | convolution fusion | flops 100859904 | bytes 1179648 | tf_op jit(solution)/shard_map/vkbz,vcz->vkbc/dot_general | solution.py:26
  52.1 0.0 copy-start.5
  52.1 0.4 convolution_convert_fusion
  52.5 0.8 copy.53
  53.3 1.6 copy.54
  54.9 0.2 copy.55
  55.1 15.3 %all_to_all.11 = bf16[32,16,128]{2,1,0:T(8,128)(2,1)S(1)} all-to-all(bf16[32,16,128]{2,1,0:T(8,128)(2,1)S(1)} %copy.55), channel_id=1, replica_groups=mesh['view'=8,'slab'=32] {'slab'}, dimensions={0} | all-to-all | bytes 262144 | tf_op jit(solution)/shard_map/all_to_all | solution.py:32
  70.4 0.7 reshape.31
  71.1 0.0 copy-done.5
  71.1 3.2 %convert_bitcast_fusion = bf16[2,4,512,512]{3,2,1,0:T(8,128)(2,1)} fusion(bf16[512,2,4,16]{3,2,1,0:T(4,128)(2,1)S(1)} %reshape.31, bf16[2,16,512]{2,1,0:T(8,128)(2,1)S(1)} %copy-done.5), kind=kOutput, calls=%fused_computation.7 | convolution fusion | flops 69206016 | bytes 4358144 | tf_op jit(solution)/shard_map/vka,bvzk->vzba/dot_general | solution.py:35
  74.3 9.5 %fusion.14 = f32[512,4,512]{0,2,1:T(8,128)} fusion(bf16[2,4,512,512]{3,2,1,0:T(8,128)(2,1)} %convert_bitcast_fusion, bf16[2,512,512]{2,1,0:T(8,128)(2,1)} %param.10, bf16[2,512,512]{2,1,0:T(8,128)(2,1)S(1)} %copy-done), kind=kOutput, calls=%fused_computation.11 | convolution fusion | flops 4297064448 | bytes 10485760 | tf_op jit(solution)/shard_map/vzya,vax->xzy/dot_general | solution.py:43
  83.8 5.5 %copy.59 = f32[512,4,512]{2,1,0:T(4,128)} copy(f32[512,4,512]{0,2,1:T(8,128)} %fusion.14) | data formatting | bytes 8388608 | tf_op jit(solution)/shard_map/vzya,vax->xzy/dot_general | solution.py:43
  89.3 0.0 copy-start.7
  89.3 0.0 copy-start.1
  89.3 0.0 all-reduce.3.cloned.1.call-update
  89.3 0.6 copy-done.7
  90.0 0.6 dynamic-slice
  91.2 71.5 %all-reduce.3.cloned.1.call-done = f32[512,4,512]{2,1,0:T(4,128)} async-done(((f32[512,4,512]{2,1,0:T(4,128)}), f32[512,4,512]{2,1,0:T(4,128)}) %all-reduce.3.cloned.1.call-update) | async-done | bytes 4194320
  162.7 1.1 constant_dynamic-slice_fusion
  163.8 0.0 copy-done.1
  163.8 2.1 %fusion.44 = f32[4,64,512]{2,1,0:T(8,128)} fusion(f32[4,64,512]{2,1,0:T(8,128)S(1)} %copy-done.1, f32[64,4,512]{2,1,0:T(4,128)S(1)} %constant_dynamic-slice_fusion, f32[4,512,512]{2,1,0:T(8,128)} %param.8, s32[]{:T(128)S(6)} %select_n.3), kind=kLoop, calls=%fused_computation.27 | loop fusion | flops 262144 | bytes 2097156 | tf_op jit(solution)/shard_map/div | solution.py:50
Async XLA Ops:
  6.5 1.2 copy-start
  6.5 7.7 %copy-start.6 = (bf16[2,512,512]{2,1,0:T(8,128)(2,1)S(1)}, bf16[2,512,512]{2,1,0:T(8,128)(2,1)}, u32[]{:S(2)}) copy-start(bf16[2,512,512]{2,1,0:T(8,128)(2,1)} %param.10) | copy-start | bytes 3145732
  6.5 7.7 %copy-start.4 = (bf16[2,16,512]{2,1,0:T(8,128)(2,1)S(1)}, bf16[2,16,512]{2,1,0:T(8,128)(2,1)}, u32[]{:S(2)}) copy-start(bf16[2,16,512]{2,1,0:T(8,128)(2,1)} %param.12) | copy-start | bytes 98308
  6.5 156.2 %all-reduce.3.cloned.1.call-start = ((), (), s32[]{:S(2)}) async-start(), calls=%async_computation.2 | async-start | bytes 8388608
  20.6 27.0 %copy-start.2 = (f32[2,128,128]{2,1,0:T(8,128)S(1)}, f32[2,128,128]{2,1,0:T(8,128)}, u32[]{:S(2)}) copy-start(f32[2,128,128]{2,1,0:T(8,128)} %param.13) | copy-start | bytes 393220
  43.4 4.2 %copy-start.3 = (f32[2,16,16,128]{3,2,1,0:T(8,128)S(1)}, f32[2,16,16,128]{3,2,1,0:T(8,128)}, u32[]{:S(2)}) copy-start(f32[2,16,16,128]{3,2,1,0:T(8,128)} %param.14) | copy-start | bytes 786436
  52.1 19.0 %copy-start.5 = (bf16[2,16,512]{2,1,0:T(8,128)(2,1)S(1)}, bf16[2,16,512]{2,1,0:T(8,128)(2,1)}, u32[]{:S(2)}) copy-start(bf16[2,16,512]{2,1,0:T(8,128)(2,1)} %param.12) | copy-start | bytes 98308
  89.3 0.7 copy-start.7
  89.3 74.5 %copy-start.1 = (f32[4,64,512]{2,1,0:T(8,128)S(1)}, f32[4,64,512]{2,1,0:T(8,128)}, u32[]{:S(2)}) copy-start(f32[4,64,512]{2,1,0:T(8,128)} %param.9) | copy-start | bytes 1572868
Sparse Core Ops, SparseCore 0:
  89.4 73.2 all-reduce.2

commit v2 on v0

v2 whole, which is shorter than its diff:
```python
import functools

import jax
import jax.numpy as jnp
from jax import lax
from jax.experimental import pallas as pl
from jax.experimental.pallas import tpu as pltpu
from jax.sharding import PartitionSpec as P

F32, BF16 = jnp.float32, jnp.bfloat16
MESH = pl.DeviceIdType.MESH
LEVELS = 32767.0


def dot(a, b, transposed=False):
    dims = (((1,), (1 if transposed else 0,)), ((), ()))
    return lax.dot_general(a, b, dims, preferred_element_type=F32)


def forward_kernel(image_ref, rx_ref, ry_ref, tof_ref, out_ref, sums):
    z = pl.program_id(0)
    views, tof = tof_ref.shape[0], tof_ref.shape[1]
    low = image_ref[0].astype(BF16)
    for v in range(views):
        along_y = dot(low, ry_ref[v]).astype(BF16)
        rotated = dot(rx_ref[v], along_y).astype(BF16)
        row = pl.multiple_of((z * views + v) * tof, tof)
        sums[pl.ds(row, tof), :] = dot(tof_ref[v], rotated)

    @pl.when(z == pl.num_programs(0) - 1)
    def _():
        out_ref[...] = sums[...].T


def forward(image, rx, ry, tof):
    own, nx, ny = image.shape
    lanes = own * tof.shape[0] * tof.shape[1]
    whole = lambda a: pl.BlockSpec(a.shape, lambda z: (0,) * a.ndim)
    return pl.pallas_call(
        forward_kernel,
        grid=(own,),
        out_shape=jax.ShapeDtypeStruct((ny, lanes), F32),
        in_specs=[pl.BlockSpec((1, nx, ny), lambda z: (z, 0, 0)), whole(rx), whole(ry), whole(tof)],
        out_specs=pl.BlockSpec((ny, lanes), lambda z: (0, 0)),
        scratch_shapes=[pltpu.VMEM((lanes, ny), F32)],
        compiler_params=pltpu.CompilerParams(vmem_limit_bytes=48 << 20),
        name="forward",
    )(image, rx, ry, tof)


def split(a):
    high = a.astype(BF16)
    return high, (a - high.astype(F32)).astype(BF16)


def three(a, b):
    (ah, al), (bh, bl) = a, b
    return dot(ah, bh) + (dot(al, bh) + dot(ah, bl))


def mix_kernel(
    sums_ref, mix_ref, mix_t_ref, background_ref, counts_ref, out_ref,
    arrived, back, wide, given, counted, staged, send_sem, recv_sem, back_send, back_recv,
):
    parts, bins, lanes = arrived.shape
    me = lax.axis_index("slab")
    barrier = pltpu.get_barrier_semaphore()

    def greet(o, carry):
        peer = lax.rem(me + o, parts)
        pl.semaphore_signal(barrier, inc=1, device_id={"slab": peer}, device_id_type=MESH)
        return carry

    lax.fori_loop(1, parts, greet, 0)
    rows = lanes // 4
    for b in range(bins):
        held = background_ref[pl.ds(b, rows, stride=bins), :]
        given[:, b * lanes:(b + 1) * lanes] = jnp.concatenate([held] * 4, axis=0).T
        held = counts_ref[pl.ds(b, rows, stride=bins), :].astype(F32)
        counted[:, b * lanes:(b + 1) * lanes] = jnp.concatenate([held] * 4, axis=0).T
    pl.semaphore_wait(barrier, parts - 1)

    def block(ref, i):
        return ref.at[pl.ds(pl.multiple_of(i * bins, bins), bins), :]

    def send(o, carry):
        peer = lax.rem(me + o, parts)
        pltpu.make_async_remote_copy(
            src_ref=block(sums_ref, peer), dst_ref=arrived.at[me], send_sem=send_sem, recv_sem=recv_sem,
            device_id={"slab": peer}, device_id_type=MESH,
        ).start()
        return carry

    lax.fori_loop(1, parts, send, 0)
    arrived[me] = block(sums_ref, me)[...]
    most = pltpu.make_async_remote_copy(
        src_ref=arrived.at[pl.ds(0, parts - 1)], dst_ref=arrived.at[pl.ds(0, parts - 1)],
        send_sem=send_sem, recv_sem=recv_sem, device_id={"slab": me}, device_id_type=MESH,
    )
    most.wait_recv()

    depth = mix_ref.shape[1]
    row = lax.broadcasted_iota(jnp.int32, (depth, lanes), 0) // parts
    lane = lax.broadcasted_iota(jnp.int32, (depth, lanes), 1)
    views = depth // (4 * parts)
    tof = rows // views
    mine = row == (lane % rows // tof) * 4 + lane // rows
    for b in range(bins):
        held = arrived[:, b, :]
        wide[:, b * lanes:(b + 1) * lanes] = jnp.where(mine, jnp.concatenate([held] * (depth // parts), axis=0), 0.0)
    mixes = split(mix_ref[...])
    mixes_t = split(mix_t_ref[...])
    step = 2 * lanes
    for b in range(0, bins, 2):
        at = slice(b * lanes, b * lanes + step)
        total = three(mixes, split(wide[:, at]))
        ratios = []
        for h in range(2):
            one = total[:, h * lanes:(h + 1) * lanes]
            one = one + pltpu.roll(one, 2 * rows, 1)
            one = one + pltpu.roll(one, rows, 1)
            inner = slice((b + h) * lanes, (b + h + 1) * lanes)
            ratios.append(counted[:, inner] / (given[:, inner] + one))
        ratios = jnp.concatenate(ratios, axis=1)
        spread = three(mixes_t, split(ratios))
        for h in range(2):
            one = jnp.where(mine, spread[:, h * lanes:(h + 1) * lanes], 0.0)
            held = one[:parts]
            for g in range(1, depth // parts):
                held = held + one[g * parts:(g + 1) * parts]
            staged[pl.ds(b + h, parts, stride=bins), :] = held
    back[...] = staged[...].astype(BF16)

    def send_back(o, carry):
        peer = lax.rem(me + o, parts)
        pltpu.make_async_remote_copy(
            src_ref=block(back, peer), dst_ref=block(out_ref, me), send_sem=back_send, recv_sem=back_recv,
            device_id={"slab": peer}, device_id_type=MESH,
        ).start()
        return carry

    lax.fori_loop(1, parts, send_back, 0)
    block(out_ref, me)[...] = block(back, me)[...]
    few = pl.ds(0, (parts - 1) * bins)
    rest = pltpu.make_async_remote_copy(
        src_ref=back.at[few, :], dst_ref=out_ref.at[few, :],
        send_sem=back_send, recv_sem=back_recv, device_id={"slab": me}, device_id_type=MESH,
    )
    rest.wait_recv()
    most.wait_send()
    rest.wait_send()


def mix_slices(sums, mix, background, counts):
    parts = lax.axis_size("slab")
    rows, lanes = sums.shape
    bins = rows // parts
    views, planes, slices = mix.shape
    own = slices // parts
    mix_t = jnp.transpose(mix.reshape(views, planes, parts, own), (0, 3, 2, 1)).reshape(views * slices, planes)
    flat = background.shape[0] * background.shape[1] * background.shape[2]
    vmem = pl.BlockSpec(memory_space=pltpu.VMEM)
    return pl.pallas_call(
        mix_kernel,
        out_shape=jax.ShapeDtypeStruct((rows, lanes), BF16),
        in_specs=[vmem] * 5,
        out_specs=vmem,
        scratch_shapes=[
            pltpu.VMEM((parts, bins, lanes), F32),
            pltpu.VMEM((rows, lanes), BF16),
            pltpu.VMEM((views * slices, bins * lanes), F32),
            pltpu.VMEM((planes, bins * lanes), F32),
            pltpu.VMEM((planes, bins * lanes), F32),
            pltpu.VMEM((rows, lanes), F32),
            pltpu.SemaphoreType.DMA,
            pltpu.SemaphoreType.DMA,
            pltpu.SemaphoreType.DMA,
            pltpu.SemaphoreType.DMA,
        ],
        compiler_params=pltpu.CompilerParams(collective_id=0, has_side_effects=True, vmem_limit_bytes=48 << 20),
        name="mix_slices",
    )(sums, mix_t.T, mix_t, background.reshape(flat, planes), counts.reshape(flat, planes))


def back_kernel(
    back_ref, image_ref, sensitivity_ref, rx_ref, ry_ref, tof_ref, out_ref,
    rx_t, tof_wide, partial, other, codes, scales, codes_in, scales_in, current,
    load_sem, pair_send, pair_recv, code_send, code_recv, scale_send, scale_recv,
):
    me = lax.axis_index("view")
    core, chip = me % 2, me // 2
    own, own_rows = sensitivity_ref.shape[0], sensitivity_ref.shape[1]
    views, tof = tof_ref.shape[0], tof_ref.shape[1]
    lanes = back_ref.shape[1]
    nx = rx_ref.shape[2]
    half = nx // 2
    chips = half // own_rows
    barrier = pltpu.get_barrier_semaphore()
    peers = [me + 1 - 2 * core] + [lax.rem(chip + o, chips) * 2 + core for o in range(1, chips)]
    for peer in peers:
        pl.semaphore_signal(barrier, inc=1, device_id={"view": peer}, device_id_type=MESH)
    load = pltpu.make_async_copy(
        image_ref.at[:, pl.ds(pl.multiple_of(me * own_rows, own_rows), own_rows), :], current, load_sem
    )
    load.start()
    for v in range(views):
        turned = rx_ref[v].T
        for c in range(2):
            for x in range(chips):
                rx_t[v, (c * chips + x) * own_rows:(c * chips + x + 1) * own_rows, :] = (
                    turned[(2 * x + c) * own_rows:(2 * x + c + 1) * own_rows]
                )
    tof_wide[...] = jnp.zeros_like(tof_wide)
    for z in range(own):
        for v in range(views):
            at = (z * views + v) * tof
            tof_wide[z * views + v, at:at + tof, :] = tof_ref[v]

    def ours(which):
        return pl.ds(pl.multiple_of(which * half, half), half)

    def pair(z):
        return pltpu.make_async_remote_copy(
            src_ref=partial.at[z, ours(1 - core), :], dst_ref=other.at[z],
            send_sem=pair_send.at[z], recv_sem=pair_recv.at[z], device_id={"view": peers[0]}, device_id_type=MESH,
        )

    def leg(z, o):
        data = pltpu.make_async_remote_copy(
            src_ref=codes.at[z, o - 1], dst_ref=codes_in.at[z, o - 1],
            send_sem=code_send.at[z, o - 1], recv_sem=code_recv.at[z, o - 1],
            device_id={"view": peers[o]}, device_id_type=MESH,
        )
        scale = pltpu.make_async_remote_copy(
            src_ref=scales.at[z, o - 1], dst_ref=scales_in.at[z, o - 1],
            send_sem=scale_send.at[z, o - 1], recv_sem=scale_recv.at[z, o - 1],
            device_id={"view": peers[o]}, device_id_type=MESH,
        )
        return data, scale

    def rows_of(o):
        at = pl.multiple_of(lax.rem(chip + o, chips) * own_rows, own_rows)
        return pl.ds(at, own_rows), pl.ds(pl.multiple_of(core * half + at, own_rows), own_rows)

    def project(z):
        total = None
        for v in range(views):
            frames = dot(back_ref[...], tof_wide[z * views + v]).astype(BF16)
            unrotated = dot(ry_ref[v], frames).astype(BF16)
            term = dot(rx_t[v], unrotated, transposed=True)
            total = term if total is None else total + term
        partial[z] = total

    def onward(z):
        pair(z).wait_recv()
        for o in (2, 1, 3):
            theirs, mine = rows_of(o)
            block = partial[z, mine, :] + other[z, theirs, :]
            top = jnp.maximum(jnp.max(jnp.abs(block), axis=0, keepdims=True), 1e-30)
            codes[z, o - 1] = jnp.round(block * (LEVELS / top)).astype(jnp.int32).astype(jnp.int16)
            scales[z, o - 1] = jnp.broadcast_to(top * (1.0 / LEVELS), scales.shape[2:])
            for copy in leg(z, o):
                copy.start()

    for z in range(own):
        project(z)
        if z == 0:
            pl.semaphore_wait(barrier, len(peers))
        pair(z).start()
        if z > 0:
            onward(z - 1)
    onward(own - 1)
    load.wait()
    for z in range(own):
        theirs, mine = rows_of(0)
        total = partial[z, mine, :] + other[z, theirs, :]
        for o in (1, 3, 2):
            for copy in leg(z, o):
                copy.wait_recv()
            total = total + codes_in[z, o - 1].astype(jnp.int32).astype(F32) * scales_in[z, o - 1][:1]
        out_ref[z] = current[z] * total / sensitivity_ref[z]
    for z in range(own):
        pair(z).wait_send()
        for o in range(1, chips):
            for copy in leg(z, o):
                copy.wait_send()


def project_back(back, image, sensitivity, rx, ry, tof):
    own, own_rows, ny = sensitivity.shape
    views, bins, nx = tof.shape
    half = nx // 2
    others = half // own_rows - 1
    vmem = pl.BlockSpec(memory_space=pltpu.VMEM)
    dma = pltpu.SemaphoreType.DMA
    return pl.pallas_call(
        back_kernel,
        out_shape=jax.ShapeDtypeStruct(sensitivity.shape, F32),
        in_specs=[vmem, pl.BlockSpec(memory_space=pl.ANY)] + [vmem] * 4,
        out_specs=vmem,
        scratch_shapes=[
            pltpu.VMEM((views, nx, nx), BF16),
            pltpu.VMEM((own * views, back.shape[1], nx), BF16),
            pltpu.VMEM((own, nx, ny), F32),
            pltpu.VMEM((own, half, ny), F32),
            pltpu.VMEM((own, others, own_rows, ny), jnp.int16),
            pltpu.VMEM((own, others, 8, ny), F32),
            pltpu.VMEM((own, others, own_rows, ny), jnp.int16),
            pltpu.VMEM((own, others, 8, ny), F32),
            pltpu.VMEM((own, own_rows, ny), F32),
            dma,
            dma((own,)), dma((own,)),
            dma((own, others)), dma((own, others)), dma((own, others)), dma((own, others)),
        ],
        compiler_params=pltpu.CompilerParams(collective_id=1, has_side_effects=True, vmem_limit_bytes=48 << 20),
        name="project_back",
    )(back, image, sensitivity, rx, ry, tof)


def local(image, sensitivity, resample_x, resample_y, tof_kernel, axial_mix, background, counts):
    sums = forward(image, resample_x, resample_y, tof_kernel)
    back = mix_slices(sums, axial_mix, background, counts)
    return project_back(back, image, sensitivity, resample_x, resample_y, tof_kernel)


def solution(mesh):
    in_specs = (
        P("slab", None, None),
        P("slab", "view", None),
        P("view", None, None),
        P("view", None, None),
        P("view", None, None),
        P("view", None, None),
        P("view", None, "slab", None),
        P("view", None, "slab", None),
    )
    out_specs = P("slab", "view", None)
    return jax.shard_map(local, mesh=mesh, in_specs=in_specs, out_specs=out_specs, check_vma=False)
```

time: 341 us -> 65.5 us (0.19)
  blocking collectives: 204 us -> 0 us
  waiting for transfers between devices: 74.9 us -> 0 us
  Pallas kernels: 0 us -> 60 us
  matrix products: 22.3 us -> 0 us
  local copies, waits for them, and re-layouts: 22.3 us -> 5.2 us
  between operations: 14.1 us -> 0.11 us
    all_to_all x2 -> x0, blocking collectives: 204 us -> none  [the longest x1 104 us: local(): lax.all_to_all(rotated, 'slab', split_axis=2, concat_axis=1, tiled=True)]
    unnamed x2 -> x0, waiting for transfers between devices: 74.9 us -> none
    pallas_call x0 -> x3, Pallas kernels: none -> 60 us  [the longest x1 27.6 us: mix_slices(): pl.pallas_call(mix_kernel, out_shape=jax.ShapeDtypeStruct((rows, lanes),...]
    dot_general x6 -> x0, matrix products: 22.3 us -> none  [the longest x1 9.19 us: local(): jnp.einsum('vzya,vax->xzy', unrotated, resample_x, preferred_element_type...]
    convert_element_type x2 -> x0, local copies, waits for them, and re-layouts: 7.82 us -> none  [the longest x1 5.42 us: local(): rotated = jnp.einsum('vzxb,vax->vzba', along_y, resample_x, preferred_ele...]
    dot_general x1 -> x0, local copies, waits for them, and re-layouts: 5.47 us -> none  [local(): jnp.einsum('vzya,vax->xzy', unrotated, resample_x, preferred_element_type...]
    all_to_all x3 -> x0, local copies, waits for them, and re-layouts: 4.5 us -> none  [the longest x1 2.45 us: local(): lax.all_to_all(spread, 'slab', split_axis=1, concat_axis=2, tiled=True)]
  transfers between devices with their start and end apart: 1 -> 0, of which waited for: 1 -> 0; matrix products, arithmetic and copies ran while one was open for 0% -> 0% of each run, Pallas kernels for 0% -> 0%
where the time goes in v2:
time: 65.5 us; the launch traced here: 65.3 us
  Pallas kernels  60 us (92%)
  local copies, waits for them, and re-layouts  5.2 us (8%)
    pallas_call x1, Pallas kernels, mix_slices(): pl.pallas_call(mix_kernel, out_shape=jax.ShapeDtypeStruct((rows, lanes),...  27.6 us
    pallas_call x1, Pallas kernels, project_back(): pl.pallas_call(back_kernel, out_shape=jax.ShapeDtypeStruct(sensitivity.sh...  24.1 us
    pallas_call x1, Pallas kernels, forward(): pl.pallas_call(forward_kernel, grid=(own,), out_shape=jax.ShapeDtypeStruc...  8.25 us
    unnamed x18, local copies, waits for them, and re-layouts  5.09 us

profile of v2, /device:TPU:1, one launch (start us, length us, event | category | flops | bytes accessed | tf_op | source)
XLA Modules:
  0.0 65.3 jit_solution(11766502879409428008)
XLA Ops:
  0.0 0.0 copy-start.5
  0.0 1.0 %copy.11 = f32[2,128,128]{1,2,0:T(8,128)S(1)} copy(f32[2,128,128]{2,1,0:T(8,128)} %param.13) | data formatting | bytes 262144 | tf_op args[5]
  1.1 0.0 copy-start.4
  1.1 0.1 copy.13.mix_ref
  1.2 0.0 copy-start
  1.2 1.2 %copy-done = bf16[2,512,512]{2,1,0:T(8,128)(2,1)S(1)} copy-done((bf16[2,512,512]{2,1,0:T(8,128)(2,1)S(1)}, bf16[2,512,512]{2,1,0:T(8,128)(2,1)}, u32[]{:S(2)}) %copy-start) | copy-done | bytes 1048600
  2.4 0.0 copy-start.2
  2.4 1.2 %copy-done.2 = bf16[2,512,512]{2,1,0:T(8,128)(2,1)S(1)} copy-done((bf16[2,512,512]{2,1,0:T(8,128)(2,1)S(1)}, bf16[2,512,512]{2,1,0:T(8,128)(2,1)}, u32[]{:S(2)}) %copy-start.2) | copy-done | bytes 1048600
  3.7 0.0 copy-start.7
  3.7 0.8 %copy-done.7 = bf16[2,16,512]{2,1,0:T(8,128)(2,1)S(1)} copy-done((bf16[2,16,512]{2,1,0:T(8,128)(2,1)S(1)}, bf16[2,16,512]{2,1,0:T(8,128)(2,1)}, u32[]{:S(2)}) %copy-start.7) | copy-done | bytes 32792
  4.4 0.0 copy-start.6
  4.4 0.0 copy-start.1
  4.4 0.0 copy-start.3
  4.4 8.3 %forward.1.sums_ref = f32[512,128]{1,0:T(8,128)S(1)} custom-call(f32[4,512,512]{2,1,0:T(8,128)} %image_ref.3, bf16[2,512,512]{2,1,0:T(8,128)(2,1)S(1)} %copy-done, bf16[2,512,512]{2,1,0:T(8,128)(2,1)S(1)} %copy-done.2, bf16[2,16,512]{2,1,0:T(8,128)(2,1)S(1)} %copy-done.7), custom_call_target="tpu_custom_call" | custom-call | tf_op jit(solution)/shard_map/forward/pallas_call | solution.py:39
  12.7 0.0 copy-done.5
  12.7 0.0 copy-done.6
  12.7 27.6 %mix_slices.1.back_ref = bf16[512,128]{1,0:T(8,128)(2,1)S(1)} custom-call(f32[512,128]{1,0:T(8,128)S(1)} %forward.1.sums_ref, f32[128,256]{1,0:T(8,128)S(1)} %copy.13.mix_ref, f32[256,128]{1,0:T(8,128)S(1)} %bitcast.9, f32[512,128]{1,0:T(8,128)S(1)} %bitcast.10, s32[512,128]{1,0:T(8,128)S(1)} %bitcast.11), custom_call_target="tpu_custom_call" | custom-call | tf_op jit(solution)/shard_map/mix_slices/pallas_call | solution.py:163
  40.3 0.0 copy-done.4
  40.3 0.0 copy-done.1
  40.3 0.0 copy-done.3
  40.4 24.1 %project_back.1 = f32[4,64,512]{2,1,0:T(8,128)S(1)} custom-call(bf16[512,128]{1,0:T(8,128)(2,1)S(1)} %mix_slices.1.back_ref, f32[4,512,512]{2,1,0:T(8,128)} %image_ref.3, f32[4,64,512]{2,1,0:T(8,128)S(1)} %copy-done.4, bf16[2,512,512]{2,1,0:T(8,128)(2,1)S(1)} %copy-done.1, bf16[2,512,512]{2,1,0:T(8,128)(2,1)S(1)} %copy-done.3, bf16[2,16,512]{2,1,0:T(8,128)(2,1)S(1)} %copy-done.7), custom_call_target="tpu_custom_call" | custom-call | tf_op jit(solution)/shard_map/project_back/pallas_call | solution.py:296
  64.5 0.8 %copy.15 = f32[4,64,512]{2,1,0:T(8,128)} copy(f32[4,64,512]{2,1,0:T(8,128)S(1)} %project_back.1) | data formatting | bytes 1048576
  (1 shorter events, 0.0 us)
Async XLA Ops:
  0.0 12.7 %copy-start.5 = (f32[2,16,16,128]{3,2,1,0:T(8,128)S(1)}, f32[2,16,16,128]{3,2,1,0:T(8,128)}, u32[]{:S(2)}) copy-start(f32[2,16,16,128]{3,2,1,0:T(8,128)} %param.14) | copy-start | bytes 786436
  1.1 39.3 %copy-start.4 = (f32[4,64,512]{2,1,0:T(8,128)S(1)}, f32[4,64,512]{2,1,0:T(8,128)}, u32[]{:S(2)}) copy-start(f32[4,64,512]{2,1,0:T(8,128)} %sensitivity_ref.1) | copy-start | bytes 1572868
  1.2 1.3 %copy-start = (bf16[2,512,512]{2,1,0:T(8,128)(2,1)S(1)}, bf16[2,512,512]{2,1,0:T(8,128)(2,1)}, u32[]{:S(2)}) copy-start(bf16[2,512,512]{2,1,0:T(8,128)(2,1)} %rx_ref.3) | copy-start | bytes 3145732
  2.4 1.2 %copy-start.2 = (bf16[2,512,512]{2,1,0:T(8,128)(2,1)S(1)}, bf16[2,512,512]{2,1,0:T(8,128)(2,1)}, u32[]{:S(2)}) copy-start(bf16[2,512,512]{2,1,0:T(8,128)(2,1)} %ry_ref.3) | copy-start | bytes 3145732
  3.7 0.8 %copy-start.7 = (bf16[2,16,512]{2,1,0:T(8,128)(2,1)S(1)}, bf16[2,16,512]{2,1,0:T(8,128)(2,1)}, u32[]{:S(2)}) copy-start(bf16[2,16,512]{2,1,0:T(8,128)(2,1)} %tof_ref.3) | copy-start | bytes 98308
  4.4 8.3 %copy-start.6 = (s32[2,16,16,128]{3,2,1,0:T(8,128)S(1)}, s32[2,16,16,128]{3,2,1,0:T(8,128)}, u32[]{:S(2)}) copy-start(s32[2,16,16,128]{3,2,1,0:T(8,128)} %param.15) | copy-start | bytes 786436
  4.4 35.9 %copy-start.1 = (bf16[2,512,512]{2,1,0:T(8,128)(2,1)S(1)}, bf16[2,512,512]{2,1,0:T(8,128)(2,1)}, u32[]{:S(2)}) copy-start(bf16[2,512,512]{2,1,0:T(8,128)(2,1)} %rx_ref.3) | copy-start | bytes 3145732
  4.4 35.9 %copy-start.3 = (bf16[2,512,512]{2,1,0:T(8,128)(2,1)S(1)}, bf16[2,512,512]{2,1,0:T(8,128)(2,1)}, u32[]{:S(2)}) copy-start(bf16[2,512,512]{2,1,0:T(8,128)(2,1)} %ry_ref.3) | copy-start | bytes 3145732

commit v3 on v0

v3 whole, which is shorter than its diff:
```python
import jax
import jax.numpy as jnp
from jax import lax
from jax.experimental import pallas as pl
from jax.experimental.pallas import tpu as pltpu
from jax.sharding import PartitionSpec as P

F32, BF16 = jnp.float32, jnp.bfloat16
MESH = pl.DeviceIdType.MESH
LEVELS = 32767.0


def dot(a, b, transposed=False):
    dims = (((1,), (1 if transposed else 0,)), ((), ()))
    return lax.dot_general(a, b, dims, preferred_element_type=F32)


def split(a):
    high = a.astype(BF16)
    return high, (a - high.astype(F32)).astype(BF16)


def kernel(
    image_hbm, sens_hbm, rx_hbm, ry_hbm, tof_hbm, mix_hbm, background_hbm, counts_hbm, out_ref,
    image, sens, rx, ry, tof_ref, mix, background, counts, current,
    sums, sending, arrived, back, back_in, wide, given, counted, staged, mix_t, mix_rows,
    rx_t, tof_wide, partial, other, codes, scales, codes_in, scales_in,
    load_sem, send_sem, recv_sem, back_send, back_recv,
    pair_send, pair_recv, code_send, code_recv, scale_send, scale_recv,
):
    own, own_rows = sens.shape[0], sens.shape[1]
    views, tof = tof_ref.shape[0], tof_ref.shape[1]
    parts, bins, lanes = arrived.shape
    nx = rx.shape[2]
    half = nx // 2
    chips = half // own_rows
    rows = views * tof
    planes = mix.shape[2]
    depth = views * own * parts
    slab = lax.axis_index("slab")
    me = lax.axis_index("view")
    core, chip = me % 2, me // 2

    loads = [
        pltpu.make_async_copy(image_hbm.at[0], image.at[0], load_sem.at[0]),
        pltpu.make_async_copy(ry_hbm, ry, load_sem.at[1]),
        pltpu.make_async_copy(rx_hbm, rx, load_sem.at[2]),
        pltpu.make_async_copy(tof_hbm, tof_ref, load_sem.at[3]),
    ]
    loads += [pltpu.make_async_copy(image_hbm.at[z], image.at[z], load_sem.at[3 + z]) for z in range(1, own)]
    late = [
        pltpu.make_async_copy(mix_hbm, mix, load_sem.at[own + 3]),
        pltpu.make_async_copy(background_hbm, background, load_sem.at[own + 4]),
        pltpu.make_async_copy(counts_hbm, counts, load_sem.at[own + 5]),
        pltpu.make_async_copy(sens_hbm, sens, load_sem.at[own + 6]),
        pltpu.make_async_copy(
            image_hbm.at[:, pl.ds(pl.multiple_of(me * own_rows, own_rows), own_rows), :], current, load_sem.at[own + 7]
        ),
    ]
    for copy in loads + late:
        copy.start()

    barrier = pltpu.get_barrier_semaphore()

    def greet(o, carry):
        peer = lax.rem(slab + o, parts)
        pl.semaphore_signal(barrier, inc=1, device_id={"slab": peer}, device_id_type=MESH)
        return carry

    lax.fori_loop(1, parts, greet, 0)
    peers = [me + 1 - 2 * core] + [lax.rem(chip + o, chips) * 2 + core for o in range(1, chips)]
    for peer in peers:
        pl.semaphore_signal(barrier, inc=1, device_id={"view": peer}, device_id_type=MESH)

    for z in range(own):
        if z == 0:
            for copy in loads[:4]:
                copy.wait()
        else:
            loads[3 + z].wait()
        low = image[z].astype(BF16)
        for v in range(views):
            along_y = dot(low, ry[v]).astype(BF16)
            rotated = dot(rx[v], along_y).astype(BF16)
            at = (z * views + v) * tof
            sums[at:at + tof, :] = dot(tof_ref[v], rotated)
    sending[...] = sums[...].T.astype(BF16)

    def block(ref, i):
        return ref.at[pl.ds(pl.multiple_of(i * bins, bins), bins), :]

    def send(o, carry):
        peer = lax.rem(slab + o, parts)
        pltpu.make_async_remote_copy(
            src_ref=block(sending, peer), dst_ref=arrived.at[slab], send_sem=send_sem, recv_sem=recv_sem,
            device_id={"slab": peer}, device_id_type=MESH,
        ).start()
        return carry

    pl.semaphore_wait(barrier, parts - 1 + len(peers))
    lax.fori_loop(1, parts, send, 0)
    arrived[slab] = block(sending, slab)[...]

    for copy in late:
        copy.wait()
    for b in range(bins):
        held = background[pl.ds(b, rows, stride=bins), :]
        given[:, b * lanes:(b + 1) * lanes] = jnp.concatenate([held] * own, axis=0).T
        held = counts[pl.ds(b, rows, stride=bins), :].astype(F32)
        counted[:, b * lanes:(b + 1) * lanes] = jnp.concatenate([held] * own, axis=0).T
    slices = own * parts
    for v in range(views):
        mix_rows[v * slices:(v + 1) * slices, :] = mix[v].T
    for v in range(views):
        for z in range(own):
            at = (v * own + z) * parts
            mix_t[at:at + parts, :] = mix_rows[pl.ds(v * slices + z, parts, stride=own), :]
    mixes_t = split(mix_t[...])
    mixes = split(mix_t[...].T)
    for v in range(views):
        turned = rx[v].T
        for c in range(2):
            for x in range(chips):
                rx_t[v, (c * chips + x) * own_rows:(c * chips + x + 1) * own_rows, :] = (
                    turned[(2 * x + c) * own_rows:(2 * x + c + 1) * own_rows]
                )
    tof_wide[...] = jnp.zeros_like(tof_wide)
    for z in range(own):
        for v in range(views):
            at = (z * views + v) * tof
            tof_wide[z * views + v, at:at + tof, :] = tof_ref[v]

    most = pltpu.make_async_remote_copy(
        src_ref=arrived.at[pl.ds(0, parts - 1)], dst_ref=arrived.at[pl.ds(0, parts - 1)],
        send_sem=send_sem, recv_sem=recv_sem, device_id={"slab": slab}, device_id_type=MESH,
    )
    most.wait_recv()

    row = lax.broadcasted_iota(jnp.int32, (depth, lanes), 0) // parts
    lane = lax.broadcasted_iota(jnp.int32, (depth, lanes), 1)
    mine = row == (lane % rows // tof) * own + lane // rows
    staged[...] = arrived[...].astype(F32).reshape(staged.shape)
    for b in range(bins):
        held = staged[pl.ds(b, parts, stride=bins), :]
        held = jnp.where(mine, jnp.concatenate([held] * (depth // parts), axis=0), 0.0)
        wide[:, b * lanes:(b + 1) * lanes] = held.astype(BF16)
    step = 2 * lanes
    for b in range(0, bins, 2):
        at = slice(b * lanes, b * lanes + step)
        total = dot(mixes[0], wide[:, at]) + dot(mixes[1], wide[:, at])
        ratios = []
        for h in range(2):
            one = total[:, h * lanes:(h + 1) * lanes]
            one = one + pltpu.roll(one, 2 * rows, 1)
            one = one + pltpu.roll(one, rows, 1)
            inner = slice((b + h) * lanes, (b + h + 1) * lanes)
            ratios.append(counted[:, inner] / (given[:, inner] + one))
        high, low = split(jnp.concatenate(ratios, axis=1))
        spread = dot(mixes_t[0], high) + (dot(mixes_t[1], high) + dot(mixes_t[0], low))
        for h in range(2):
            one = jnp.where(mine, spread[:, h * lanes:(h + 1) * lanes], 0.0)
            held = one[:parts]
            for g in range(1, depth // parts):
                held = held + one[g * parts:(g + 1) * parts]
            staged[pl.ds(b + h, parts, stride=bins), :] = held
    back[...] = staged[...].astype(BF16)

    def send_back(o, carry):
        peer = lax.rem(slab + o, parts)
        pltpu.make_async_remote_copy(
            src_ref=block(back, peer), dst_ref=block(back_in, slab), send_sem=back_send, recv_sem=back_recv,
            device_id={"slab": peer}, device_id_type=MESH,
        ).start()
        return carry

    lax.fori_loop(1, parts, send_back, 0)
    block(back_in, slab)[...] = block(back, slab)[...]
    few = pl.ds(0, (parts - 1) * bins)
    rest = pltpu.make_async_remote_copy(
        src_ref=back.at[few, :], dst_ref=back_in.at[few, :],
        send_sem=back_send, recv_sem=back_recv, device_id={"slab": slab}, device_id_type=MESH,
    )
    rest.wait_recv()

    def ours(which):
        return pl.ds(pl.multiple_of(which * half, half), half)

    def pair(z):
        return pltpu.make_async_remote_copy(
            src_ref=partial.at[z, ours(1 - core), :], dst_ref=other.at[z],
            send_sem=pair_send.at[z], recv_sem=pair_recv.at[z], device_id={"view": peers[0]}, device_id_type=MESH,
        )

    def leg(z, o):
        data = pltpu.make_async_remote_copy(
            src_ref=codes.at[z, o - 1], dst_ref=codes_in.at[z, o - 1],
            send_sem=code_send.at[z, o - 1], recv_sem=code_recv.at[z, o - 1],
            device_id={"view": peers[o]}, device_id_type=MESH,
        )
        scale = pltpu.make_async_remote_copy(
            src_ref=scales.at[z, o - 1], dst_ref=scales_in.at[z, o - 1],
            send_sem=scale_send.at[z, o - 1], recv_sem=scale_recv.at[z, o - 1],
            device_id={"view": peers[o]}, device_id_type=MESH,
        )
        return data, scale

    def rows_of(o):
        at = pl.multiple_of(lax.rem(chip + o, chips) * own_rows, own_rows)
        return pl.ds(at, own_rows), pl.ds(pl.multiple_of(core * half + at, own_rows), own_rows)

    def project(z):
        total = None
        for v in range(views):
            frames = dot(back_in[...], tof_wide[z * views + v]).astype(BF16)
            unrotated = dot(ry[v], frames).astype(BF16)
            term = dot(rx_t[v], unrotated, transposed=True)
            total = term if total is None else total + term
        partial[z] = total

    def onward(z):
        pair(z).wait_recv()
        for o in (2, 1, 3):
            theirs, ours_at = rows_of(o)
            held = partial[z, ours_at, :] + other[z, theirs, :]
            top = jnp.maximum(jnp.max(jnp.abs(held), axis=0, keepdims=True), 1e-30)
            codes[z, o - 1] = jnp.round(held * (LEVELS / top)).astype(jnp.int32).astype(jnp.int16)
            scales[z, o - 1] = top * (1.0 / LEVELS)
            for copy in leg(z, o):
                copy.start()

    for z in range(own):
        project(z)
        pair(z).start()
        if z > 0:
            onward(z - 1)
    onward(own - 1)
    for z in range(own):
        theirs, ours_at = rows_of(0)
        total = partial[z, ours_at, :] + other[z, theirs, :]
        for o in (1, 3, 2):
            for copy in leg(z, o):
                copy.wait_recv()
            total = total + codes_in[z, o - 1].astype(jnp.int32).astype(F32) * scales_in[z, o - 1]
        out_ref[z] = current[z] * total / sens[z]
    most.wait_send()
    rest.wait_send()
    for z in range(own):
        pair(z).wait_send()
        for o in range(1, chips):
            for copy in leg(z, o):
                copy.wait_send()


def local(image, sensitivity, resample_x, resample_y, tof_kernel, axial_mix, background, counts):
    parts = lax.axis_size("slab")
    own, own_rows, ny = sensitivity.shape
    views, tof, nx = tof_kernel.shape
    bins, planes = background.shape[2:]
    lanes = own * views * tof
    half = nx // 2
    others = half // own_rows - 1
    flat = views * tof * bins
    vm, dma, i32, i16 = pltpu.VMEM, pltpu.SemaphoreType.DMA, jnp.int32, jnp.int16
    hbm = pl.BlockSpec(memory_space=pl.ANY)
    return pl.pallas_call(
        kernel,
        out_shape=jax.ShapeDtypeStruct(sensitivity.shape, F32),
        in_specs=[hbm] * 8,
        out_specs=pl.BlockSpec(memory_space=pltpu.VMEM),
        scratch_shapes=[
            vm(image.shape, F32), vm(sensitivity.shape, F32),
            vm(resample_x.shape, BF16), vm(resample_y.shape, BF16), vm(tof_kernel.shape, BF16),
            vm(axial_mix.shape, F32), vm((flat, planes), F32), vm((flat, planes), i32),
            vm(sensitivity.shape, F32),
            vm((lanes, ny), F32), vm((ny, lanes), BF16), vm((parts, bins, lanes), BF16),
            vm((ny, lanes), BF16), vm((ny, lanes), BF16),
            vm((views * own * parts, bins * lanes), BF16),
            vm((planes, bins * lanes), F32), vm((planes, bins * lanes), F32),
            vm((ny, lanes), F32),
            vm((views * own * parts, planes), F32), vm((views * own * parts, planes), F32),
            vm((views, nx, nx), BF16), vm((own * views, lanes, nx), BF16),
            vm((own, nx, ny), F32), vm((own, half, ny), F32),
            vm((own, others, own_rows, ny), i16), vm((own, others, 1, ny), F32),
            vm((own, others, own_rows, ny), i16), vm((own, others, 1, ny), F32),
            dma((own + 8,)), dma, dma, dma, dma,
            dma((own,)), dma((own,)),
            dma((own, others)), dma((own, others)), dma((own, others)), dma((own, others)),
        ],
        compiler_params=pltpu.CompilerParams(collective_id=0, has_side_effects=True, vmem_limit_bytes=56 << 20),
        name="update",
    )(
        image, sensitivity, resample_x, resample_y, tof_kernel, axial_mix,
        background.reshape(flat, planes), counts.reshape(flat, planes),
    )


def solution(mesh):
    in_specs = (
        P("slab", None, None),
        P("slab", "view", None),
        P("view", None, None),
        P("view", None, None),
        P("view", None, None),
        P("view", None, None),
        P("view", None, "slab", None),
        P("view", None, "slab", None),
    )
    out_specs = P("slab", "view", None)
    return jax.shard_map(local, mesh=mesh, in_specs=in_specs, out_specs=out_specs, check_vma=False)
```

time: 341 us -> 51.8 us (0.15)
  blocking collectives: 204 us -> 0 us
  waiting for transfers between devices: 74.9 us -> 0 us
  Pallas kernels: 0 us -> 49.8 us
  matrix products: 22.3 us -> 0 us
  local copies, waits for them, and re-layouts: 22.3 us -> 1.87 us
  between operations: 14.1 us -> 0.01 us
    all_to_all x2 -> x0, blocking collectives: 204 us -> none  [the longest x1 104 us: local(): lax.all_to_all(rotated, 'slab', split_axis=2, concat_axis=1, tiled=True)]
    unnamed x2 -> x0, waiting for transfers between devices: 74.9 us -> none
    pallas_call x0 -> x1, Pallas kernels: none -> 49.8 us  [local(): pl.pallas_call(kernel, out_shape=jax.ShapeDtypeStruct(sensitivity.shape,...]
    dot_general x6 -> x0, matrix products: 22.3 us -> none  [the longest x1 9.19 us: local(): jnp.einsum('vzya,vax->xzy', unrotated, resample_x, preferred_element_type...]
    convert_element_type x2 -> x0, local copies, waits for them, and re-layouts: 7.82 us -> none  [the longest x1 5.42 us: local(): rotated = jnp.einsum('vzxb,vax->vzba', along_y, resample_x, preferred_ele...]
    dot_general x1 -> x0, local copies, waits for them, and re-layouts: 5.47 us -> none  [local(): jnp.einsum('vzya,vax->xzy', unrotated, resample_x, preferred_element_type...]
    all_to_all x3 -> x0, local copies, waits for them, and re-layouts: 4.5 us -> none  [the longest x1 2.45 us: local(): lax.all_to_all(spread, 'slab', split_axis=1, concat_axis=2, tiled=True)]
  transfers between devices with their start and end apart: 1 -> 0, of which waited for: 1 -> 0; matrix products, arithmetic and copies ran while one was open for 0% -> 0% of each run, Pallas kernels for 0% -> 0%
where the time goes in v3:
time: 51.8 us; the launch traced here: 51.7 us
  Pallas kernels  49.8 us (96%)
  local copies, waits for them, and re-layouts  1.87 us (4%)
    pallas_call x1, Pallas kernels, local(): pl.pallas_call(kernel, out_shape=jax.ShapeDtypeStruct(sensitivity.shape,...  49.8 us
    unnamed x1, local copies, waits for them, and re-layouts  1.87 us

profile of v3, /device:TPU:1, one launch (start us, length us, event | category | flops | bytes accessed | tf_op | source)
XLA Modules:
  0.0 51.7 jit_solution(16284758074888829771)
XLA Ops:
  0.0 49.8 %update.1 = f32[4,64,512]{2,1,0:T(8,128)} custom-call(f32[4,512,512]{2,1,0:T(8,128)} %image_hbm.1, f32[4,64,512]{2,1,0:T(8,128)} %sens_hbm.1, bf16[2,512,512]{2,1,0:T(8,128)(2,1)} %rx_hbm.1, bf16[2,512,512]{2,1,0:T(8,128)(2,1)} %ry_hbm.1, bf16[2,16,512]{2,1,0:T(8,128)(2,1)} %tof_hbm.1, f32[2,128,128]{2,1,0:T(8,128)} %mix_hbm.1, f32[512,128]{1,0:T(8,128)} %bitcast.2, ...), custom_call_target="tpu_custom_call" | custom-call | tf_op jit(solution)/shard_map/update/pallas_call | solution.py:265
  49.8 1.9 %copy.10 = f32[4,64,512]{2,1,0:T(8,128)} copy(f32[4,64,512]{2,1,0:T(8,128)} %update.1) | data formatting | bytes 1048576

commit v4 on v3

--- a/solution.py
+++ b/solution.py
@@ -36,7 +36,6 @@
     chips = half // own_rows
     rows = views * tof
     planes = mix.shape[2]
-    depth = views * own * parts
     slab = lax.axis_index("slab")
     me = lax.axis_index("view")
     core, chip = me % 2, me // 2
@@ -103,11 +102,12 @@
 
     for copy in late:
         copy.wait()
-    for b in range(bins):
-        held = background[pl.ds(b, rows, stride=bins), :]
-        given[:, b * lanes:(b + 1) * lanes] = jnp.concatenate([held] * own, axis=0).T
-        held = counts[pl.ds(b, rows, stride=bins), :].astype(F32)
-        counted[:, b * lanes:(b + 1) * lanes] = jnp.concatenate([held] * own, axis=0).T
+    for b in range(0, bins, own):
+        at = slice(b // own * lanes, (b // own + 1) * lanes)
+        held = [background[pl.ds(b + g, rows, stride=bins), :] for g in range(own)]
+        given[:, at] = jnp.concatenate(held, axis=0).T
+        held = [counts[pl.ds(b + g, rows, stride=bins), :].astype(F32) for g in range(own)]
+        counted[:, at] = jnp.concatenate(held, axis=0).T
     slices = own * parts
     for v in range(views):
         mix_rows[v * slices:(v + 1) * slices, :] = mix[v].T
@@ -136,33 +136,45 @@
     )
     most.wait_recv()
 
-    row = lax.broadcasted_iota(jnp.int32, (depth, lanes), 0) // parts
-    lane = lax.broadcasted_iota(jnp.int32, (depth, lanes), 1)
-    mine = row == (lane % rows // tof) * own + lane // rows
+    group = lax.broadcasted_iota(jnp.int32, (parts, lanes), 1) // rows
+    view_of = lax.broadcasted_iota(jnp.int32, (parts, lanes), 1) % rows // tof
+
+    def swap(held):
+        step = own // 2
+        while step:
+            swapped = list(held)
+            low = group // step % 2 == 0
+            for g in range(own):
+                if g // step % 2 == 0:
+                    a, b = held[g], held[g + step]
+                    swapped[g] = jnp.where(low, a, pltpu.roll(b, step * rows, 1))
+                    swapped[g + step] = jnp.where(low, pltpu.roll(a, lanes - step * rows, 1), b)
+            held, step = swapped, step // 2
+        return held
+
     staged[...] = arrived[...].astype(F32).reshape(staged.shape)
-    for b in range(bins):
-        held = staged[pl.ds(b, parts, stride=bins), :]
-        held = jnp.where(mine, jnp.concatenate([held] * (depth // parts), axis=0), 0.0)
-        wide[:, b * lanes:(b + 1) * lanes] = held.astype(BF16)
-    step = 2 * lanes
-    for b in range(0, bins, 2):
-        at = slice(b * lanes, b * lanes + step)
-        total = dot(mixes[0], wide[:, at]) + dot(mixes[1], wide[:, at])
-        ratios = []
-        for h in range(2):
-            one = total[:, h * lanes:(h + 1) * lanes]
-            one = one + pltpu.roll(one, 2 * rows, 1)
-            one = one + pltpu.roll(one, rows, 1)
-            inner = slice((b + h) * lanes, (b + h + 1) * lanes)
-            ratios.append(counted[:, inner] / (given[:, inner] + one))
-        high, low = split(jnp.concatenate(ratios, axis=1))
-        spread = dot(mixes_t[0], high) + (dot(mixes_t[1], high) + dot(mixes_t[0], low))
-        for h in range(2):
-            one = jnp.where(mine, spread[:, h * lanes:(h + 1) * lanes], 0.0)
-            held = one[:parts]
-            for g in range(1, depth // parts):
-                held = held + one[g * parts:(g + 1) * parts]
-            staged[pl.ds(b + h, parts, stride=bins), :] = held
+    for b in range(0, bins, own):
+        at = slice(b // own * lanes, (b // own + 1) * lanes)
+        held = swap([staged[pl.ds(b + g, parts, stride=bins), :] for g in range(own)])
+        for v in range(views):
+            for z in range(own):
+                row = (v * own + z) * parts
+                wide[row:row + parts, at] = jnp.where(view_of == v, held[z], 0.0).astype(BF16)
+    total = dot(mixes[0], wide[...]) + dot(mixes[1], wide[...])
+    high, low = split(counted[...] / (given[...] + total))
+    spread = dot(mixes_t[0], high) + (dot(mixes_t[1], high) + dot(mixes_t[0], low))
+    for b in range(0, bins, own):
+        at = slice(b // own * lanes, (b // own + 1) * lanes)
+        held = []
+        for z in range(own):
+            one = spread[z * parts:(z + 1) * parts, at]
+            for v in range(1, views):
+                row = (v * own + z) * parts
+                one = jnp.where(view_of == v, spread[row:row + parts, at], one)
+            held.append(one)
+        held = swap(held)
+        for g in range(own):
+            staged[pl.ds(b + g, parts, stride=bins), :] = held[g]
     back[...] = staged[...].astype(BF16)
 
     def send_back(o, carry):
@@ -261,7 +273,7 @@
     others = half // own_rows - 1
     flat = views * tof * bins
     vm, dma, i32, i16 = pltpu.VMEM, pltpu.SemaphoreType.DMA, jnp.int32, jnp.int16
-    hbm = pl.BlockSpec(memory_space=pl.ANY)
+    hbm = pl.BlockSpec(memory_space=pltpu.HBM)
     return pl.pallas_call(
         kernel,
         out_shape=jax.ShapeDtypeStruct(sensitivity.shape, F32),
@@ -274,8 +286,8 @@
             vm(sensitivity.shape, F32),
             vm((lanes, ny), F32), vm((ny, lanes), BF16), vm((parts, bins, lanes), BF16),
             vm((ny, lanes), BF16), vm((ny, lanes), BF16),
-            vm((views * own * parts, bins * lanes), BF16),
-            vm((planes, bins * lanes), F32), vm((planes, bins * lanes), F32),
+            vm((views * own * parts, bins // own * lanes), BF16),
+            vm((planes, bins // own * lanes), F32), vm((planes, bins // own * lanes), F32),
             vm((ny, lanes), F32),
             vm((views * own * parts, planes), F32), vm((views * own * parts, planes), F32),
             vm((views, nx, nx), BF16), vm((own * views, lanes, nx), BF16),

time: 51.8 us -> 50.2 us (0.969)
  Pallas kernels: 49.8 us -> 48.2 us
    pallas_call x1, Pallas kernels: 49.8 us -> 48.2 us  [local(): pl.pallas_call(kernel, out_shape=jax.ShapeDtypeStruct(sensitivity.shape,...]
where the time goes in v4:
time: 50.2 us; the launch traced here: 50.1 us
  Pallas kernels  48.2 us (96%)
  local copies, waits for them, and re-layouts  1.87 us (4%)
    pallas_call x1, Pallas kernels, local(): pl.pallas_call(kernel, out_shape=jax.ShapeDtypeStruct(sensitivity.shape,...  48.2 us
    unnamed x1, local copies, waits for them, and re-layouts  1.87 us

profile of v4, /device:TPU:1, one launch (start us, length us, event | category | flops | bytes accessed | tf_op | source)
XLA Modules:
  0.0 50.1 jit_solution(19311043176578290)
XLA Ops:
  0.0 48.2 %update.1 = f32[4,64,512]{2,1,0:T(8,128)} custom-call(f32[4,512,512]{2,1,0:T(8,128)} %image_hbm.1, f32[4,64,512]{2,1,0:T(8,128)} %sens_hbm.1, bf16[2,512,512]{2,1,0:T(8,128)(2,1)} %rx_hbm.1, bf16[2,512,512]{2,1,0:T(8,128)(2,1)} %ry_hbm.1, bf16[2,16,512]{2,1,0:T(8,128)(2,1)} %tof_hbm.1, f32[2,128,128]{2,1,0:T(8,128)} %mix_hbm.1, f32[512,128]{1,0:T(8,128)} %bitcast.2, ...), custom_call_target="tpu_custom_call" | custom-call | tf_op jit(solution)/shard_map/update/pallas_call | solution.py:277
  48.2 1.9 %copy.10 = f32[4,64,512]{2,1,0:T(8,128)} copy(f32[4,64,512]{2,1,0:T(8,128)} %update.1) | data formatting | bytes 1048576

commit v5 on v4

--- a/solution.py
+++ b/solution.py
@@ -7,7 +7,7 @@
 
 F32, BF16 = jnp.float32, jnp.bfloat16
 MESH = pl.DeviceIdType.MESH
-LEVELS = 32767.0
+PAD = 16
 
 
 def dot(a, b, transposed=False):
@@ -23,27 +23,28 @@
 def kernel(
     image_hbm, sens_hbm, rx_hbm, ry_hbm, tof_hbm, mix_hbm, background_hbm, counts_hbm, out_ref,
     image, sens, rx, ry, tof_ref, mix, background, counts, current,
-    sums, sending, arrived, back, back_in, wide, given, counted, staged, mix_t, mix_rows,
-    rx_t, tof_wide, partial, other, codes, scales, codes_in, scales_in,
+    sums, sending, arrived, back, back_all, wide, given, counted, staged, mix_t, mix_rows,
+    rx_near, tof_tall, tof_near, lines, partial, other,
     load_sem, send_sem, recv_sem, back_send, back_recv,
-    pair_send, pair_recv, code_send, code_recv, scale_send, scale_recv,
+    pair_send, pair_recv, band_send, band_recv, share_send, share_recv,
 ):
     own, own_rows = sens.shape[0], sens.shape[1]
     views, tof = tof_ref.shape[0], tof_ref.shape[1]
     parts, bins, lanes = arrived.shape
     nx = rx.shape[2]
-    half = nx // 2
-    chips = half // own_rows
+    chips = back_all.shape[0]
+    width = nx // chips
+    reach = rx_near.shape[2]
     rows = views * tof
-    planes = mix.shape[2]
     slab = lax.axis_index("slab")
     me = lax.axis_index("view")
     core, chip = me % 2, me // 2
+    inner = slice(PAD, PAD + nx)
 
     loads = [
         pltpu.make_async_copy(image_hbm.at[0], image.at[0], load_sem.at[0]),
-        pltpu.make_async_copy(ry_hbm, ry, load_sem.at[1]),
-        pltpu.make_async_copy(rx_hbm, rx, load_sem.at[2]),
+        pltpu.make_async_copy(ry_hbm, ry.at[0, :, inner, :], load_sem.at[1]),
+        pltpu.make_async_copy(rx_hbm, rx.at[:, inner, :], load_sem.at[2]),
         pltpu.make_async_copy(tof_hbm, tof_ref, load_sem.at[3]),
     ]
     loads += [pltpu.make_async_copy(image_hbm.at[z], image.at[z], load_sem.at[3 + z]) for z in range(1, own)]
@@ -68,21 +69,63 @@
 
     lax.fori_loop(1, parts, greet, 0)
     peers = [me + 1 - 2 * core] + [lax.rem(chip + o, chips) * 2 + core for o in range(1, chips)]
+    for edge in (slice(0, PAD), slice(PAD + nx, PAD + nx + PAD)):
+        tof_tall[edge, :] = jnp.zeros((PAD, lanes), BF16)
+        for v in range(views):
+            rx[v, edge, :] = jnp.zeros((PAD, nx), BF16)
+            ry[0, v, edge, :] = jnp.zeros((PAD, nx), BF16)
+    for o in range(1, chips):
+        ry[o] = jnp.zeros(ry.shape[1:], BF16)
     for peer in peers:
         pl.semaphore_signal(barrier, inc=1, device_id={"view": peer}, device_id_type=MESH)
 
+    def near(which):
+        at = pl.multiple_of(which * width, width)
+        return pl.ds(at, reach), pl.ds(at, width)
+
+    def bands(o):
+        target = dict(device_id={"view": peers[o]}, device_id_type=MESH)
+        there, across = near(peers[o] // 2)
+        pieces = [
+            (rx.at[:, there, across], rx_near.at[o]),
+            (tof_tall.at[there, :], tof_near.at[o]),
+        ]
+        for b in range(chips):
+            at = (slice(None), slice(b * width, b * width + reach), slice(b * width, (b + 1) * width))
+            pieces.append((ry.at[(0,) + at], ry.at[(o,) + at]))
+        return [
+            pltpu.make_async_remote_copy(
+                src_ref=a, dst_ref=b, send_sem=band_send.at[o - 1, n], recv_sem=band_recv.at[o - 1, n], **target
+            )
+            for n, (a, b) in enumerate(pieces)
+        ]
+
+    here, along = near(chip)
+    mine_near = [
+        pltpu.make_async_copy(rx.at[:, here, along], rx_near.at[0], load_sem.at[0]),
+        pltpu.make_async_copy(tof_tall.at[here, :], tof_near.at[0], load_sem.at[1]),
+    ]
     for z in range(own):
         if z == 0:
             for copy in loads[:4]:
                 copy.wait()
+            tall = jnp.concatenate([tof_ref[...].astype(F32).reshape(rows, nx)] * own, axis=0)
+            tof_tall[inner, :] = tall.T.astype(BF16)
+            for copy in mine_near:
+                copy.start()
         else:
             loads[3 + z].wait()
         low = image[z].astype(BF16)
         for v in range(views):
-            along_y = dot(low, ry[v]).astype(BF16)
-            rotated = dot(rx[v], along_y).astype(BF16)
+            along_y = dot(low, ry[0, v, inner, :]).astype(BF16)
+            rotated = dot(rx[v, inner, :], along_y).astype(BF16)
             at = (z * views + v) * tof
             sums[at:at + tof, :] = dot(tof_ref[v], rotated)
+        if z == own // 2 - 1:
+            pl.semaphore_wait(barrier, parts - 1 + len(peers))
+            for o in (1, 3, 2):
+                for copy in bands(o):
+                    copy.start()
     sending[...] = sums[...].T.astype(BF16)
 
     def block(ref, i):
@@ -96,7 +139,6 @@
         ).start()
         return carry
 
-    pl.semaphore_wait(barrier, parts - 1 + len(peers))
     lax.fori_loop(1, parts, send, 0)
     arrived[slab] = block(sending, slab)[...]
 
@@ -117,18 +159,8 @@
             mix_t[at:at + parts, :] = mix_rows[pl.ds(v * slices + z, parts, stride=own), :]
     mixes_t = split(mix_t[...])
     mixes = split(mix_t[...].T)
-    for v in range(views):
-        turned = rx[v].T
-        for c in range(2):
-            for x in range(chips):
-                rx_t[v, (c * chips + x) * own_rows:(c * chips + x + 1) * own_rows, :] = (
-                    turned[(2 * x + c) * own_rows:(2 * x + c + 1) * own_rows]
-                )
-    tof_wide[...] = jnp.zeros_like(tof_wide)
-    for z in range(own):
-        for v in range(views):
-            at = (z * views + v) * tof
-            tof_wide[z * views + v, at:at + tof, :] = tof_ref[v]
+    for copy in mine_near:
+        copy.wait()
 
     most = pltpu.make_async_remote_copy(
         src_ref=arrived.at[pl.ds(0, parts - 1)], dst_ref=arrived.at[pl.ds(0, parts - 1)],
@@ -180,87 +212,67 @@
     def send_back(o, carry):
         peer = lax.rem(slab + o, parts)
         pltpu.make_async_remote_copy(
-            src_ref=block(back, peer), dst_ref=block(back_in, slab), send_sem=back_send, recv_sem=back_recv,
+            src_ref=block(back, peer), dst_ref=block(back_all.at[0], slab), send_sem=back_send, recv_sem=back_recv,
             device_id={"slab": peer}, device_id_type=MESH,
         ).start()
         return carry
 
     lax.fori_loop(1, parts, send_back, 0)
-    block(back_in, slab)[...] = block(back, slab)[...]
+    block(back_all.at[0], slab)[...] = block(back, slab)[...]
     few = pl.ds(0, (parts - 1) * bins)
     rest = pltpu.make_async_remote_copy(
-        src_ref=back.at[few, :], dst_ref=back_in.at[few, :],
+        src_ref=back.at[few, :], dst_ref=back_all.at[0, few, :],
         send_sem=back_send, recv_sem=back_recv, device_id={"slab": slab}, device_id_type=MESH,
     )
     rest.wait_recv()
 
-    def ours(which):
-        return pl.ds(pl.multiple_of(which * half, half), half)
+    def share(o):
+        return pltpu.make_async_remote_copy(
+            src_ref=back_all.at[0], dst_ref=back_all.at[o], send_sem=share_send.at[o - 1], recv_sem=share_recv.at[o - 1],
+            device_id={"view": peers[o]}, device_id_type=MESH,
+        )
+
+    for o in (1, 3, 2):
+        share(o).start()
+    part = lax.broadcasted_iota(jnp.int32, (reach, lanes), 1) // tof
+    for o in (0, 1, 3, 2):
+        if o:
+            for copy in bands(o):
+                copy.wait_recv()
+            share(o).wait_recv()
+        weights = tof_near[o].astype(F32)
+        for v in range(views):
+            chosen = [jnp.where(part == z * views + v, weights, 0.0).astype(BF16) for z in range(own)]
+            frames = dot(jnp.concatenate(chosen, axis=0), back_all[o], transposed=True).astype(BF16)
+            unrotated = dot(frames, ry[o, v, inner, :], transposed=True).astype(BF16)
+            at = (o * views + v) * reach
+            for z in range(own):
+                lines[z, at:at + reach, :] = unrotated[z * reach:(z + 1) * reach]
+
+    def half(which):
+        return pl.ds(pl.multiple_of(which * own_rows, own_rows), own_rows)
 
     def pair(z):
         return pltpu.make_async_remote_copy(
-            src_ref=partial.at[z, ours(1 - core), :], dst_ref=other.at[z],
+            src_ref=partial.at[z, half(1 - core), :], dst_ref=other.at[z],
             send_sem=pair_send.at[z], recv_sem=pair_recv.at[z], device_id={"view": peers[0]}, device_id_type=MESH,
         )
 
-    def leg(z, o):
-        data = pltpu.make_async_remote_copy(
-            src_ref=codes.at[z, o - 1], dst_ref=codes_in.at[z, o - 1],
-            send_sem=code_send.at[z, o - 1], recv_sem=code_recv.at[z, o - 1],
-            device_id={"view": peers[o]}, device_id_type=MESH,
-        )
-        scale = pltpu.make_async_remote_copy(
-            src_ref=scales.at[z, o - 1], dst_ref=scales_in.at[z, o - 1],
-            send_sem=scale_send.at[z, o - 1], recv_sem=scale_recv.at[z, o - 1],
-            device_id={"view": peers[o]}, device_id_type=MESH,
-        )
-        return data, scale
-
-    def rows_of(o):
-        at = pl.multiple_of(lax.rem(chip + o, chips) * own_rows, own_rows)
-        return pl.ds(at, own_rows), pl.ds(pl.multiple_of(core * half + at, own_rows), own_rows)
-
-    def project(z):
-        total = None
-        for v in range(views):
-            frames = dot(back_in[...], tof_wide[z * views + v]).astype(BF16)
-            unrotated = dot(ry[v], frames).astype(BF16)
-            term = dot(rx_t[v], unrotated, transposed=True)
-            total = term if total is None else total + term
-        partial[z] = total
-
-    def onward(z):
+    turned = rx_near[...].reshape(chips * views * reach, width).T
+    for z in range(own):
+        partial[z] = dot(turned, lines[z])
+        pair(z).start()
+    for z in range(own):
         pair(z).wait_recv()
-        for o in (2, 1, 3):
-            theirs, ours_at = rows_of(o)
-            held = partial[z, ours_at, :] + other[z, theirs, :]
-            top = jnp.maximum(jnp.max(jnp.abs(held), axis=0, keepdims=True), 1e-30)
-            codes[z, o - 1] = jnp.round(held * (LEVELS / top)).astype(jnp.int32).astype(jnp.int16)
-            scales[z, o - 1] = top * (1.0 / LEVELS)
-            for copy in leg(z, o):
-                copy.start()
-
-    for z in range(own):
-        project(z)
-        pair(z).start()
-        if z > 0:
-            onward(z - 1)
-    onward(own - 1)
-    for z in range(own):
-        theirs, ours_at = rows_of(0)
-        total = partial[z, ours_at, :] + other[z, theirs, :]
-        for o in (1, 3, 2):
-            for copy in leg(z, o):
-                copy.wait_recv()
-            total = total + codes_in[z, o - 1].astype(jnp.int32).astype(F32) * scales_in[z, o - 1]
-        out_ref[z] = current[z] * total / sens[z]
+        out_ref[z] = current[z] * (partial[z, half(core), :] + other[z]) / sens[z]
     most.wait_send()
     rest.wait_send()
     for z in range(own):
         pair(z).wait_send()
-        for o in range(1, chips):
-            for copy in leg(z, o):
-                copy.wait_send()
+    for o in range(1, chips):
+        share(o).wait_send()
+        for copy in bands(o):
+            copy.wait_send()
 
 
 def local(image, sensitivity, resample_x, resample_y, tof_kernel, axial_mix, background, counts):
@@ -269,10 +281,11 @@
     views, tof, nx = tof_kernel.shape
     bins, planes = background.shape[2:]
     lanes = own * views * tof
-    half = nx // 2
-    others = half // own_rows - 1
+    chips = lax.axis_size("view") // 2
+    width = nx // chips
+    reach = width + 2 * PAD
     flat = views * tof * bins
-    vm, dma, i32, i16 = pltpu.VMEM, pltpu.SemaphoreType.DMA, jnp.int32, jnp.int16
+    vm, dma, i32 = pltpu.VMEM, pltpu.SemaphoreType.DMA, jnp.int32
     hbm = pl.BlockSpec(memory_space=pltpu.HBM)
     return pl.pallas_call(
         kernel,
@@ -281,22 +294,20 @@
         out_specs=pl.BlockSpec(memory_space=pltpu.VMEM),
         scratch_shapes=[
             vm(image.shape, F32), vm(sensitivity.shape, F32),
-            vm(resample_x.shape, BF16), vm(resample_y.shape, BF16), vm(tof_kernel.shape, BF16),
+            vm((views, nx + 2 * PAD, nx), BF16), vm((chips, views, nx + 2 * PAD, nx), BF16), vm(tof_kernel.shape, BF16),
             vm(axial_mix.shape, F32), vm((flat, planes), F32), vm((flat, planes), i32),
             vm(sensitivity.shape, F32),
             vm((lanes, ny), F32), vm((ny, lanes), BF16), vm((parts, bins, lanes), BF16),
-            vm((ny, lanes), BF16), vm((ny, lanes), BF16),
+            vm((ny, lanes), BF16), vm((chips, ny, lanes), BF16),
             vm((views * own * parts, bins // own * lanes), BF16),
             vm((planes, bins // own * lanes), F32), vm((planes, bins // own * lanes), F32),
             vm((ny, lanes), F32),
             vm((views * own * parts, planes), F32), vm((views * own * parts, planes), F32),
-            vm((views, nx, nx), BF16), vm((own * views, lanes, nx), BF16),
-            vm((own, nx, ny), F32), vm((own, half, ny), F32),
-            vm((own, others, own_rows, ny), i16), vm((own, others, 1, ny), F32),
-            vm((own, others, own_rows, ny), i16), vm((own, others, 1, ny), F32),
+            vm((chips, views, reach, width), BF16), vm((nx + 2 * PAD, lanes), BF16), vm((chips, reach, lanes), BF16),
+            vm((own, chips * views * reach, ny), BF16), vm((own, width, ny), F32), vm((own, own_rows, ny), F32),
             dma((own + 8,)), dma, dma, dma, dma,
             dma((own,)), dma((own,)),
-            dma((own, others)), dma((own, others)), dma((own, others)), dma((own, others)),
+            dma((chips - 1, chips + 2)), dma((chips - 1, chips + 2)), dma((chips - 1,)), dma((chips - 1,)),
         ],
         compiler_params=pltpu.CompilerParams(collective_id=0, has_side_effects=True, vmem_limit_bytes=56 << 20),
         name="update",

time: 50.2 us -> 46.8 us (0.932)
  Pallas kernels: 48.2 us -> 44.8 us
    pallas_call x1, Pallas kernels: 48.2 us -> 44.8 us  [local(): pl.pallas_call(kernel, out_shape=jax.ShapeDtypeStruct(sensitivity.shape,...]
where the time goes in v5:
time: 46.8 us; the launch traced here: 46.7 us
  Pallas kernels  44.8 us (96%)
  local copies, waits for them, and re-layouts  1.87 us (4%)
    pallas_call x1, Pallas kernels, local(): pl.pallas_call(kernel, out_shape=jax.ShapeDtypeStruct(sensitivity.shape,...  44.8 us
    unnamed x1, local copies, waits for them, and re-layouts  1.87 us

profile of v5, /device:TPU:1, one launch (start us, length us, event | category | flops | bytes accessed | tf_op | source)
XLA Modules:
  0.0 46.7 jit_solution(3991953353873079802)
XLA Ops:
  0.0 44.8 %update.1 = f32[4,64,512]{2,1,0:T(8,128)} custom-call(f32[4,512,512]{2,1,0:T(8,128)} %image_hbm.1, f32[4,64,512]{2,1,0:T(8,128)} %sens_hbm.1, bf16[2,512,512]{2,1,0:T(8,128)(2,1)} %rx_hbm.1, bf16[2,512,512]{2,1,0:T(8,128)(2,1)} %ry_hbm.1, bf16[2,16,512]{2,1,0:T(8,128)(2,1)} %tof_hbm.1, f32[2,128,128]{2,1,0:T(8,128)} %mix_hbm.1, f32[512,128]{1,0:T(8,128)} %bitcast.2, ...), custom_call_target="tpu_custom_call" | custom-call | tf_op jit(solution)/shard_map/update/pallas_call | solution.py:290
  44.9 1.9 %copy.10 = f32[4,64,512]{2,1,0:T(8,128)} copy(f32[4,64,512]{2,1,0:T(8,128)} %update.1) | data formatting | bytes 1048576

commit v6 on v5

--- a/solution.py
+++ b/solution.py
@@ -8,6 +8,8 @@
 F32, BF16 = jnp.float32, jnp.bfloat16
 MESH = pl.DeviceIdType.MESH
 PAD = 16
+PIECE = 2 * PAD
+RING = 8
 
 
 def dot(a, b, transposed=False):
@@ -24,7 +26,7 @@
     image_hbm, sens_hbm, rx_hbm, ry_hbm, tof_hbm, mix_hbm, background_hbm, counts_hbm, out_ref,
     image, sens, rx, ry, tof_ref, mix, background, counts, current,
     sums, sending, arrived, back, back_all, wide, given, counted, staged, mix_t, mix_rows,
-    rx_near, tof_tall, tof_near, lines, partial, other,
+    rx_near, tof_tall, tof_near, rx_pack, ry_pack, rx_in, ry_in, lines, partial, other,
     load_sem, send_sem, recv_sem, back_send, back_recv,
     pair_send, pair_recv, band_send, band_recv, share_send, share_recv,
 ):
@@ -74,8 +76,6 @@
         for v in range(views):
             rx[v, edge, :] = jnp.zeros((PAD, nx), BF16)
             ry[0, v, edge, :] = jnp.zeros((PAD, nx), BF16)
-    for o in range(1, chips):
-        ry[o] = jnp.zeros(ry.shape[1:], BF16)
     for peer in peers:
         pl.semaphore_signal(barrier, inc=1, device_id={"view": peer}, device_id_type=MESH)
 
@@ -85,20 +85,37 @@
 
     def bands(o):
         target = dict(device_id={"view": peers[o]}, device_id_type=MESH)
-        there, across = near(peers[o] // 2)
+        to = peers[o] // 2
         pieces = [
-            (rx.at[:, there, across], rx_near.at[o]),
-            (tof_tall.at[there, :], tof_near.at[o]),
+            (rx_pack.at[to], rx_in.at[o - 1]),
+            (tof_tall.at[near(to)[0], :], tof_near.at[o]),
+            (ry_pack, ry_in.at[o - 1]),
         ]
-        for b in range(chips):
-            at = (slice(None), slice(b * width, b * width + reach), slice(b * width, (b + 1) * width))
-            pieces.append((ry.at[(0,) + at], ry.at[(o,) + at]))
         return [
             pltpu.make_async_remote_copy(
                 src_ref=a, dst_ref=b, send_sem=band_send.at[o - 1, n], recv_sem=band_recv.at[o - 1, n], **target
             )
             for n, (a, b) in enumerate(pieces)
         ]
+
+    part = lax.broadcasted_iota(jnp.int32, (PIECE, width), 1) // PIECE
+    keep = [jnp.where(part == g, 1.0, 0.0).astype(BF16) for g in range(width // PIECE)]
+
+    def pack(ref, b):
+        cols = slice(b * width, (b + 1) * width)
+        halves = []
+        for h in range(2):
+            rows_at = [b * width + (g + h) * PIECE for g in range(len(keep))]
+            halves.append(sum(ref[r:r + PIECE, cols] * m for r, m in zip(rows_at, keep)))
+        return jnp.concatenate(halves, axis=0)
+
+    def unpack(held):
+        first, second = held[:PIECE], held[PIECE:]
+        rows_of = [first * keep[0]]
+        for g in range(1, len(keep)):
+            rows_of.append(first * keep[g] + second * keep[g - 1])
+        rows_of.append(second * keep[-1])
+        return jnp.concatenate(rows_of, axis=0)
 
     here, along = near(chip)
     mine_near = [
@@ -113,6 +130,10 @@
             tof_tall[inner, :] = tall.T.astype(BF16)
             for copy in mine_near:
                 copy.start()
+            for b in range(chips):
+                for v in range(views):
+                    rx_pack[b, v] = pack(rx.at[v], b)
+                    ry_pack[b, v] = pack(ry.at[0, v], b)
         else:
             loads[3 + z].wait()
         low = image[z].astype(BF16)
@@ -131,15 +152,19 @@
     def block(ref, i):
         return ref.at[pl.ds(pl.multiple_of(i * bins, bins), bins), :]
 
-    def send(o, carry):
-        peer = lax.rem(slab + o, parts)
+    rings = parts // RING
+    far = [(dy, dz) for dy in range(rings) for dz in range(RING) if dy or dz]
+    far.sort(key=lambda d: -min(d[0], rings - d[0]) - min(d[1], RING - d[1]))
+
+    def peer_at(dy, dz):
+        return lax.rem(slab // RING + dy, rings) * RING + lax.rem(slab + dz, RING)
+
+    for dy, dz in far:
+        peer = peer_at(dy, dz)
         pltpu.make_async_remote_copy(
             src_ref=block(sending, peer), dst_ref=arrived.at[slab], send_sem=send_sem, recv_sem=recv_sem,
             device_id={"slab": peer}, device_id_type=MESH,
         ).start()
-        return carry
-
-    lax.fori_loop(1, parts, send, 0)
     arrived[slab] = block(sending, slab)[...]
 
     for copy in late:
@@ -161,6 +186,9 @@
     mixes = split(mix_t[...].T)
     for copy in mine_near:
         copy.wait()
+    for o in range(1, chips):
+        for v in range(views):
+            ry[o, v] = jnp.zeros(ry.shape[2:], BF16)
 
     most = pltpu.make_async_remote_copy(
         src_ref=arrived.at[pl.ds(0, parts - 1)], dst_ref=arrived.at[pl.ds(0, parts - 1)],
@@ -209,16 +237,21 @@
             staged[pl.ds(b + g, parts, stride=bins), :] = held[g]
     back[...] = staged[...].astype(BF16)
 
-    def send_back(o, carry):
-        peer = lax.rem(slab + o, parts)
+    for dy, dz in far:
+        peer = peer_at(dy, dz)
         pltpu.make_async_remote_copy(
             src_ref=block(back, peer), dst_ref=block(back_all.at[0], slab), send_sem=back_send, recv_sem=back_recv,
             device_id={"slab": peer}, device_id_type=MESH,
         ).start()
-        return carry
-
-    lax.fori_loop(1, parts, send_back, 0)
     block(back_all.at[0], slab)[...] = block(back, slab)[...]
+    for o in (1, 3, 2):
+        for copy in bands(o):
+            copy.wait_recv()
+        for v in range(views):
+            rx_near[o, v] = unpack(rx_in[o - 1, v])
+            for b in range(chips):
+                ry[o, v, b * width:b * width + reach, b * width:(b + 1) * width] = unpack(ry_in[o - 1, b, v])
+    turned = rx_near[...].reshape(chips * views * reach, width).T
     few = pl.ds(0, (parts - 1) * bins)
     rest = pltpu.make_async_remote_copy(
         src_ref=back.at[few, :], dst_ref=back_all.at[0, few, :],
@@ -234,23 +267,21 @@
 
     for o in (1, 3, 2):
         share(o).start()
-    part = lax.broadcasted_iota(jnp.int32, (reach, lanes), 1) // tof
+    which = lax.broadcasted_iota(jnp.int32, (reach, lanes), 1) // tof
     for o in (0, 1, 3, 2):
         if o:
-            for copy in bands(o):
-                copy.wait_recv()
             share(o).wait_recv()
         weights = tof_near[o].astype(F32)
         for v in range(views):
-            chosen = [jnp.where(part == z * views + v, weights, 0.0).astype(BF16) for z in range(own)]
+            chosen = [jnp.where(which == z * views + v, weights, 0.0).astype(BF16) for z in range(own)]
             frames = dot(jnp.concatenate(chosen, axis=0), back_all[o], transposed=True).astype(BF16)
             unrotated = dot(frames, ry[o, v, inner, :], transposed=True).astype(BF16)
             at = (o * views + v) * reach
             for z in range(own):
                 lines[z, at:at + reach, :] = unrotated[z * reach:(z + 1) * reach]
 
-    def half(which):
-        return pl.ds(pl.multiple_of(which * own_rows, own_rows), own_rows)
+    def half(at):
+        return pl.ds(pl.multiple_of(at * own_rows, own_rows), own_rows)
 
     def pair(z):
         return pltpu.make_async_remote_copy(
@@ -258,7 +289,6 @@
             send_sem=pair_send.at[z], recv_sem=pair_recv.at[z], device_id={"view": peers[0]}, device_id_type=MESH,
         )
 
-    turned = rx_near[...].reshape(chips * views * reach, width).T
     for z in range(own):
         partial[z] = dot(turned, lines[z])
         pair(z).start()
@@ -304,10 +334,12 @@
             vm((ny, lanes), F32),
             vm((views * own * parts, planes), F32), vm((views * own * parts, planes), F32),
             vm((chips, views, reach, width), BF16), vm((nx + 2 * PAD, lanes), BF16), vm((chips, reach, lanes), BF16),
+            vm((chips, views, 2 * PIECE, width), BF16), vm((chips, views, 2 * PIECE, width), BF16),
+            vm((chips - 1, views, 2 * PIECE, width), BF16), vm((chips - 1, chips, views, 2 * PIECE, width), BF16),
             vm((own, chips * views * reach, ny), BF16), vm((own, width, ny), F32), vm((own, own_rows, ny), F32),
             dma((own + 8,)), dma, dma, dma, dma,
             dma((own,)), dma((own,)),
-            dma((chips - 1, chips + 2)), dma((chips - 1, chips + 2)), dma((chips - 1,)), dma((chips - 1,)),
+            dma((chips - 1, 3)), dma((chips - 1, 3)), dma((chips - 1,)), dma((chips - 1,)),
         ],
         compiler_params=pltpu.CompilerParams(collective_id=0, has_side_effects=True, vmem_limit_bytes=56 << 20),
         name="update",

time: 46.8 us -> 42.9 us (0.917)
  Pallas kernels: 44.8 us -> 40.9 us
    pallas_call x1, Pallas kernels: 44.8 us -> 40.9 us  [local(): pl.pallas_call(kernel, out_shape=jax.ShapeDtypeStruct(sensitivity.shape,...]
where the time goes in v6:
time: 42.9 us; the launch traced here: 42.8 us
  Pallas kernels  40.9 us (95%)
  local copies, waits for them, and re-layouts  1.87 us (4%)
    pallas_call x1, Pallas kernels, local(): pl.pallas_call(kernel, out_shape=jax.ShapeDtypeStruct(sensitivity.shape,...  40.9 us
    unnamed x1, local copies, waits for them, and re-layouts  1.87 us

profile of v6, /device:TPU:1, one launch (start us, length us, event | category | flops | bytes accessed | tf_op | source)
XLA Modules:
  0.0 42.8 jit_solution(8812854086703001534)
XLA Ops:
  0.0 40.9 %update.1 = f32[4,64,512]{2,1,0:T(8,128)} custom-call(f32[4,512,512]{2,1,0:T(8,128)} %image_hbm.1, f32[4,64,512]{2,1,0:T(8,128)} %sens_hbm.1, bf16[2,512,512]{2,1,0:T(8,128)(2,1)} %rx_hbm.1, bf16[2,512,512]{2,1,0:T(8,128)(2,1)} %ry_hbm.1, bf16[2,16,512]{2,1,0:T(8,128)(2,1)} %tof_hbm.1, f32[2,128,128]{2,1,0:T(8,128)} %mix_hbm.1, f32[512,128]{1,0:T(8,128)} %bitcast.2, ...), custom_call_target="tpu_custom_call" | custom-call | tf_op jit(solution)/shard_map/update/pallas_call | solution.py:320
  40.9 1.9 %copy.10 = f32[4,64,512]{2,1,0:T(8,128)} copy(f32[4,64,512]{2,1,0:T(8,128)} %update.1) | data formatting | bytes 1048576

commit v7 on v6

--- a/solution.py
+++ b/solution.py
@@ -341,12 +341,15 @@
             dma((own,)), dma((own,)),
             dma((chips - 1, 3)), dma((chips - 1, 3)), dma((chips - 1,)), dma((chips - 1,)),
         ],
-        compiler_params=pltpu.CompilerParams(collective_id=0, has_side_effects=True, vmem_limit_bytes=56 << 20),
+        compiler_params=pltpu.CompilerParams(collective_id=0, has_side_effects=True, vmem_limit_bytes=48 << 20),
         name="update",
-    )(
-        image, sensitivity, resample_x, resample_y, tof_kernel, axial_mix,
-        background.reshape(flat, planes), counts.reshape(flat, planes),
-    )
+    )(*[
+        pltpu.with_memory_space_constraint(a, pltpu.HBM)
+        for a in (
+            image, sensitivity, resample_x, resample_y, tof_kernel, axial_mix,
+            background.reshape(flat, planes), counts.reshape(flat, planes),
+        )
+    ])
 
 
 def solution(mesh):

time: 42.9 us -> 41.1 us (0.958)
  local copies, waits for them, and re-layouts: 1.87 us -> 0.8 us
  Pallas kernels: 40.9 us -> 40.2 us
    unnamed x1, local copies, waits for them, and re-layouts: 1.87 us -> 0.8 us
    pallas_call x1, Pallas kernels: 40.9 us -> 40.2 us  [local(): pl.pallas_call(kernel, out_shape=jax.ShapeDtypeStruct(sensitivity.shape,...]
where the time goes in v7:
time: 41.1 us; the launch traced here: 41 us
  Pallas kernels  40.2 us (98%)
  local copies, waits for them, and re-layouts  0.8 us (2%)
    pallas_call x1, Pallas kernels, local(): pl.pallas_call(kernel, out_shape=jax.ShapeDtypeStruct(sensitivity.shape,...  40.2 us

profile of v7, /device:TPU:1, one launch (start us, length us, event | category | flops | bytes accessed | tf_op | source)
XLA Modules:
  0.0 41.0 jit_solution(3013813531559092287)
XLA Ops:
  0.0 40.2 %update.1 = f32[4,64,512]{2,1,0:T(8,128)S(1)} custom-call(f32[4,512,512]{2,1,0:T(8,128)} %image_hbm.1, f32[4,64,512]{2,1,0:T(8,128)} %sens_hbm.1, bf16[2,512,512]{2,1,0:T(8,128)(2,1)} %rx_hbm.1, bf16[2,512,512]{2,1,0:T(8,128)(2,1)} %ry_hbm.1, bf16[2,16,512]{2,1,0:T(8,128)(2,1)} %tof_hbm.1, f32[2,128,128]{2,1,0:T(8,128)} %mix_hbm.1, f32[512,128]{1,0:T(8,128)} %bitcast.2, ...), custom_call_target="tpu_custom_call" | custom-call | tf_op jit(solution)/shard_map/update/pallas_call | solution.py:320
  40.3 0.8 %copy.10 = f32[4,64,512]{2,1,0:T(8,128)} copy(f32[4,64,512]{2,1,0:T(8,128)S(1)} %update.1) | data formatting | bytes 1048576

commit v8 on v7

v8 whole, which is shorter than its diff:
```python
import jax
import jax.numpy as jnp
from jax import lax
from jax.experimental import pallas as pl
from jax.experimental.pallas import tpu as pltpu
from jax.sharding import PartitionSpec as P

F32, BF16 = jnp.float32, jnp.bfloat16
MESH = pl.DeviceIdType.MESH
PAD = 16
PIECE = 2 * PAD
RING = 8


def dot(a, b, transposed=False):
    dims = (((1,), (1 if transposed else 0,)), ((), ()))
    return lax.dot_general(a, b, dims, preferred_element_type=F32)


def split(a):
    high = a.astype(BF16)
    return high, (a - high.astype(F32)).astype(BF16)


def kernel(
    image_hbm, sens_hbm, rx_hbm, ry_hbm, tof_hbm, mix_hbm, background_hbm, counts_hbm, out_ref,
    image, sens, rx, ry, tof_ref, mix, background, counts, current,
    sums, sending, arrived, back, back_all, wide, given, counted, staged, mix_t, mix_rows,
    rx_near, tof_tall, tof_near, rx_pack, ry_pack, rx_in, ry_in, lines, partial, other,
    load_sem, send_sem, recv_sem, back_send, back_recv,
    pair_send, pair_recv, band_send, band_recv, share_send, share_recv,
):
    own, own_rows = sens.shape[0], sens.shape[1]
    views, tof = tof_ref.shape[0], tof_ref.shape[1]
    parts, rank, lanes = arrived.shape[1:]
    bins = 2 * rank
    nx = rx.shape[2]
    chips = back_all.shape[0]
    width = nx // chips
    reach = rx_near.shape[2]
    slab = lax.axis_index("slab")
    me = lax.axis_index("view")
    core, chip = me % 2, me // 2
    inner = slice(PAD, PAD + nx)

    loads = [
        pltpu.make_async_copy(image_hbm.at[0], image.at[0], load_sem.at[0]),
        pltpu.make_async_copy(ry_hbm, ry.at[0, :, inner, :], load_sem.at[1]),
        pltpu.make_async_copy(rx_hbm, rx.at[:, inner, :], load_sem.at[2]),
        pltpu.make_async_copy(tof_hbm, tof_ref, load_sem.at[3]),
    ]
    loads += [pltpu.make_async_copy(image_hbm.at[z], image.at[z], load_sem.at[3 + z]) for z in range(1, own)]
    late = [
        pltpu.make_async_copy(mix_hbm, mix, load_sem.at[own + 3]),
        pltpu.make_async_copy(background_hbm, background, load_sem.at[own + 4]),
        pltpu.make_async_copy(counts_hbm, counts, load_sem.at[own + 5]),
        pltpu.make_async_copy(sens_hbm, sens, load_sem.at[own + 6]),
        pltpu.make_async_copy(
            image_hbm.at[:, pl.ds(pl.multiple_of(me * own_rows, own_rows), own_rows), :], current, load_sem.at[own + 7]
        ),
    ]
    for copy in loads + late:
        copy.start()

    barrier = pltpu.get_barrier_semaphore()

    def greet(o, carry):
        peer = lax.rem(slab + o, parts)
        pl.semaphore_signal(barrier, inc=1, device_id={"slab": peer}, device_id_type=MESH)
        return carry

    lax.fori_loop(1, parts, greet, 0)
    peers = [me + 1 - 2 * core] + [lax.rem(chip + o, chips) * 2 + core for o in range(1, chips)]
    for edge in (slice(0, PAD), slice(PAD + nx, PAD + nx + PAD)):
        tof_tall[edge, :] = jnp.zeros((PAD, lanes), BF16)
        for v in range(views):
            rx[v, edge, :] = jnp.zeros((PAD, nx), BF16)
            ry[0, v, edge, :] = jnp.zeros((PAD, nx), BF16)
    for peer in peers:
        pl.semaphore_signal(barrier, inc=1, device_id={"view": peer}, device_id_type=MESH)

    def near(which):
        at = pl.multiple_of(which * width, width)
        return pl.ds(at, reach), pl.ds(at, width)

    def bands(o):
        target = dict(device_id={"view": peers[o]}, device_id_type=MESH)
        to = peers[o] // 2
        pieces = [
            (rx_pack.at[to], rx_in.at[o - 1]),
            (tof_tall.at[near(to)[0], :], tof_near.at[o]),
            (ry_pack, ry_in.at[o - 1]),
        ]
        return [
            pltpu.make_async_remote_copy(
                src_ref=a, dst_ref=b, send_sem=band_send.at[o - 1, n], recv_sem=band_recv.at[o - 1, n], **target
            )
            for n, (a, b) in enumerate(pieces)
        ]

    part = lax.broadcasted_iota(jnp.int32, (PIECE, width), 1) // PIECE
    keep = [jnp.where(part == g, 1.0, 0.0).astype(BF16) for g in range(width // PIECE)]

    def pack(ref, b):
        cols = slice(b * width, (b + 1) * width)
        halves = []
        for h in range(2):
            rows_at = [b * width + (g + h) * PIECE for g in range(len(keep))]
            halves.append(sum(ref[r:r + PIECE, cols] * m for r, m in zip(rows_at, keep)))
        return jnp.concatenate(halves, axis=0)

    def unpack(held):
        first, second = held[:PIECE], held[PIECE:]
        rows_of = [first * keep[0]]
        for g in range(1, len(keep)):
            rows_of.append(first * keep[g] + second * keep[g - 1])
        rows_of.append(second * keep[-1])
        return jnp.concatenate(rows_of, axis=0)

    here, along = near(chip)
    mine_near = [
        pltpu.make_async_copy(rx.at[:, here, along], rx_near.at[0], load_sem.at[0]),
        pltpu.make_async_copy(tof_tall.at[here, :], tof_near.at[0], load_sem.at[1]),
    ]
    rings = parts // RING
    far = [(dy, dz) for dy in range(rings) for dz in range(RING) if dy or dz]
    far.sort(key=lambda d: -min(d[0], rings - d[0]) - min(d[1], RING - d[1]))

    def peer_at(dy, dz):
        return lax.rem(slab // RING + dy, rings) * RING + lax.rem(slab + dz, RING)

    def block(ref, i):
        return ref.at[i]

    def send(v):
        for dy, dz in far:
            peer = peer_at(dy, dz)
            pltpu.make_async_remote_copy(
                src_ref=block(sending.at[v], peer), dst_ref=arrived.at[v, slab],
                send_sem=send_sem.at[v], recv_sem=recv_sem.at[v],
                device_id={"slab": peer}, device_id_type=MESH,
            ).start()
        arrived[v, slab] = block(sending.at[v], slab)[...]

    def sent(v):
        most = arrived.at[v, pl.ds(0, parts - 1)]
        return pltpu.make_async_remote_copy(
            src_ref=most, dst_ref=most, send_sem=send_sem.at[v], recv_sem=recv_sem.at[v],
            device_id={"slab": slab}, device_id_type=MESH,
        )

    def send_back(v):
        for dy, dz in far:
            peer = peer_at(dy, dz)
            pltpu.make_async_remote_copy(
                src_ref=block(back.at[v], peer), dst_ref=block(back_all.at[0, v], slab),
                send_sem=back_send.at[v], recv_sem=back_recv.at[v],
                device_id={"slab": peer}, device_id_type=MESH,
            ).start()
        block(back_all.at[0, v], slab)[...] = block(back.at[v], slab)[...]

    def sent_back(v):
        few = pl.ds(0, parts - 1)
        return pltpu.make_async_remote_copy(
            src_ref=back.at[v, few], dst_ref=back_all.at[0, v, few],
            send_sem=back_send.at[v], recv_sem=back_recv.at[v],
            device_id={"slab": slab}, device_id_type=MESH,
        )

    side = lax.broadcasted_iota(jnp.int32, (parts, rank, lanes), 2) < lanes // 2
    for v in range(views):
        for z in range(own):
            if v == 0 and z == 0:
                for copy in loads[:4]:
                    copy.wait()
                tall = [tof_ref[u].astype(F32) for u in range(views) for n in range(own)]
                tof_tall[inner, :] = jnp.concatenate(tall, axis=0).T.astype(BF16)
                for copy in mine_near:
                    copy.start()
                for b in range(chips):
                    for u in range(views):
                        rx_pack[b, u] = pack(rx.at[u], b)
                        ry_pack[b, u] = pack(ry.at[0, u], b)
            elif v == 0:
                loads[3 + z].wait()
            low = image[z].astype(BF16)
            along_y = dot(low, ry[0, v, inner, :]).astype(BF16)
            rotated = dot(rx[v, inner, :], along_y).astype(BF16)
            held = dot(tof_ref[v], rotated)
            for h in range(2):
                at = (h * own + z) * tof
                sums[at:at + tof, :] = held
        held = sums[...].T.reshape(parts, bins, lanes)
        held = jnp.where(side, held[:, :rank], held[:, rank:])
        sending[v] = held.astype(BF16)
        if v == 0:
            pl.semaphore_wait(barrier, parts - 1 + len(peers))
        send(v)
        if v == 0:
            for o in (1, 3, 2):
                for copy in bands(o):
                    copy.start()

    for copy in late:
        copy.wait()
    runs = rank // own
    for v in range(views):
        for n in range(runs):
            at = slice(n * lanes, (n + 1) * lanes)
            first = [v * tof * bins + h * rank + n * own + g for h in range(2) for g in range(own)]
            held = [background[pl.ds(b, tof, stride=bins), :] for b in first]
            given[v, :, at] = jnp.concatenate(held, axis=0).T
            held = [counts[pl.ds(b, tof, stride=bins), :].astype(F32) for b in first]
            counted[v, :, at] = jnp.concatenate(held, axis=0).T
    slices = own * parts
    for v in range(views):
        mix_rows[v * slices:(v + 1) * slices, :] = mix[v].T
    for v in range(views):
        for z in range(own):
            at = (v * own + z) * parts
            mix_t[at:at + parts, :] = mix_rows[pl.ds(v * slices + z, parts, stride=own), :]
    mixes_t = [split(mix_t[v * slices:(v + 1) * slices, :]) for v in range(views)]
    mixes = [split(mix_t[v * slices:(v + 1) * slices, :].T) for v in range(views)]
    for copy in mine_near:
        copy.wait()
    group = lax.broadcasted_iota(jnp.int32, (parts, lanes), 1) // tof

    def swap(held):
        step = own // 2
        while step:
            swapped = list(held)
            low = group // step % 2 == 0
            for g in range(own):
                if g // step % 2 == 0:
                    a, b = held[g], held[g + step]
                    swapped[g] = jnp.where(low, a, pltpu.roll(b, step * tof, 1))
                    swapped[g + step] = jnp.where(low, pltpu.roll(a, lanes - step * tof, 1), b)
            held, step = swapped, step // 2
        return held

    for v in range(views):
        sent(v).wait_recv()
        staged[...] = arrived[v].astype(F32).reshape(staged.shape)
        for n in range(runs):
            at = slice(n * lanes, (n + 1) * lanes)
            held = swap([staged[pl.ds(n * own + g, parts, stride=rank), :] for g in range(own)])
            for z in range(own):
                wide[z * parts:(z + 1) * parts, at] = held[z].astype(BF16)
        total = dot(mixes[v][0], wide[...]) + dot(mixes[v][1], wide[...])
        high, low = split(counted[v] / (given[v] + total))
        spread = dot(mixes_t[v][0], high) + (dot(mixes_t[v][1], high) + dot(mixes_t[v][0], low))
        for n in range(runs):
            at = slice(n * lanes, (n + 1) * lanes)
            held = swap([spread[z * parts:(z + 1) * parts, at] for z in range(own)])
            for g in range(own):
                staged[pl.ds(n * own + g, parts, stride=rank), :] = held[g]
        back[v] = staged[...].reshape(parts, rank, lanes).astype(BF16)
        send_back(v)
    for o in range(1, chips):
        for v in range(views):
            ry[o, v] = jnp.zeros(ry.shape[2:], BF16)
    for o in (1, 3, 2):
        for copy in bands(o):
            copy.wait_recv()
        for v in range(views):
            rx_near[o, v] = unpack(rx_in[o - 1, v])
            for b in range(chips):
                ry[o, v, b * width:b * width + reach, b * width:(b + 1) * width] = unpack(ry_in[o - 1, b, v])
    turned = rx_near[...].reshape(chips * views * reach, width).T
    def share(o, v):
        return pltpu.make_async_remote_copy(
            src_ref=back_all.at[0, v], dst_ref=back_all.at[o, v],
            send_sem=share_send.at[o - 1, v], recv_sem=share_recv.at[o - 1, v],
            device_id={"view": peers[o]}, device_id_type=MESH,
        )

    which = lax.broadcasted_iota(jnp.int32, (reach, lanes), 1) // tof

    def project(o, v):
        if o:
            share(o, v).wait_recv()
        held = back_all[o, v].astype(F32).reshape(parts * rank, lanes)
        turn = pltpu.roll(held, lanes // 2, 1)
        pair_of = [held, turn] if v == 0 else [turn, held]
        pair_of = [h.reshape(parts, rank, lanes) for h in pair_of]
        spread_out = jnp.concatenate(pair_of, axis=1).reshape(parts * bins, lanes).astype(BF16)
        weights = tof_near[o].astype(F32)
        chosen = [jnp.where(which == v * own + z, weights, 0.0).astype(BF16) for z in range(own)]
        frames = dot(jnp.concatenate(chosen, axis=0), spread_out, transposed=True).astype(BF16)
        unrotated = dot(frames, ry[o, v, inner, :], transposed=True).astype(BF16)
        at = (o * views + v) * reach
        for z in range(own):
            lines[z, at:at + reach, :] = unrotated[z * reach:(z + 1) * reach]

    for v in range(views):
        sent_back(v).wait_recv()
        for o in (1, 3, 2):
            share(o, v).start()
        project(0, v)
    for v in range(views):
        for o in (1, 3, 2):
            project(o, v)

    def half(at):
        return pl.ds(pl.multiple_of(at * own_rows, own_rows), own_rows)

    def pair(z):
        return pltpu.make_async_remote_copy(
            src_ref=partial.at[z, half(1 - core), :], dst_ref=other.at[z],
            send_sem=pair_send.at[z], recv_sem=pair_recv.at[z], device_id={"view": peers[0]}, device_id_type=MESH,
        )

    for z in range(own):
        partial[z] = dot(turned, lines[z])
        pair(z).start()
    for z in range(own):
        pair(z).wait_recv()
        out_ref[z] = current[z] * (partial[z, half(core), :] + other[z]) / sens[z]
    for v in range(views):
        sent(v).wait_send()
        sent_back(v).wait_send()
    for z in range(own):
        pair(z).wait_send()
    for o in range(1, chips):
        for v in range(views):
            share(o, v).wait_send()
        for copy in bands(o):
            copy.wait_send()


def local(image, sensitivity, resample_x, resample_y, tof_kernel, axial_mix, background, counts):
    parts = lax.axis_size("slab")
    own, own_rows, ny = sensitivity.shape
    views, tof, nx = tof_kernel.shape
    bins, planes = background.shape[2:]
    lanes = own * views * tof
    chips = lax.axis_size("view") // 2
    width = nx // chips
    reach = width + 2 * PAD
    flat = views * tof * bins
    packed = ny // 2
    columns = bins * tof
    vm, dma, i32 = pltpu.VMEM, pltpu.SemaphoreType.DMA, jnp.int32
    hbm = pl.BlockSpec(memory_space=pltpu.HBM)
    return pl.pallas_call(
        kernel,
        out_shape=jax.ShapeDtypeStruct(sensitivity.shape, F32),
        in_specs=[hbm] * 8,
        out_specs=pl.BlockSpec(memory_space=pltpu.VMEM),
        scratch_shapes=[
            vm(image.shape, F32), vm(sensitivity.shape, F32),
            vm((views, nx + 2 * PAD, nx), BF16), vm((chips, views, nx + 2 * PAD, nx), BF16), vm(tof_kernel.shape, BF16),
            vm(axial_mix.shape, F32), vm((flat, planes), F32), vm((flat, planes), i32),
            vm(sensitivity.shape, F32),
            vm((lanes, ny), F32), vm((views, parts, bins // 2, lanes), BF16), vm((views, parts, bins // 2, lanes), BF16),
            vm((views, parts, bins // 2, lanes), BF16), vm((chips, views, parts, bins // 2, lanes), BF16),
            vm((own * parts, columns), BF16),
            vm((views, planes, columns), F32), vm((views, planes, columns), F32),
            vm((packed, lanes), F32),
            vm((views * own * parts, planes), F32), vm((views * own * parts, planes), F32),
            vm((chips, views, reach, width), BF16), vm((nx + 2 * PAD, lanes), BF16), vm((chips, reach, lanes), BF16),
            vm((chips, views, 2 * PIECE, width), BF16), vm((chips, views, 2 * PIECE, width), BF16),
            vm((chips - 1, views, 2 * PIECE, width), BF16), vm((chips - 1, chips, views, 2 * PIECE, width), BF16),
            vm((own, chips * views * reach, ny), BF16), vm((own, width, ny), F32), vm((own, own_rows, ny), F32),
            dma((own + 8,)), dma((views,)), dma((views,)), dma((views,)), dma((views,)),
            dma((own,)), dma((own,)),
            dma((chips - 1, 3)), dma((chips - 1, 3)), dma((chips - 1, views)), dma((chips - 1, views)),
        ],
        compiler_params=pltpu.CompilerParams(collective_id=0, has_side_effects=True, vmem_limit_bytes=48 << 20),
        name="update",
    )(*[
        pltpu.with_memory_space_constraint(a, pltpu.HBM)
        for a in (
            image, sensitivity, resample_x, resample_y, tof_kernel, axial_mix,
            background.reshape(flat, planes), counts.reshape(flat, planes),
        )
    ])


def solution(mesh):
    in_specs = (
        P("slab", None, None),
        P("slab", "view", None),
        P("view", None, None),
        P("view", None, None),
        P("view", None, None),
        P("view", None, None),
        P("view", None, "slab", None),
        P("view", None, "slab", None),
    )
    out_specs = P("slab", "view", None)
    return jax.shard_map(local, mesh=mesh, in_specs=in_specs, out_specs=out_specs, check_vma=False)
```

time: 41.1 us -> 37.9 us (0.922)
  Pallas kernels: 40.2 us -> 37 us
    pallas_call x1, Pallas kernels: 40.2 us -> 37 us  [local(): pl.pallas_call(kernel, out_shape=jax.ShapeDtypeStruct(sensitivity.shape,...]
where the time goes in v8:
time: 37.9 us
  Pallas kernels  37 us (98%)
  local copies, waits for them, and re-layouts  0.8 us (2%)
    pallas_call x1, Pallas kernels, local(): pl.pallas_call(kernel, out_shape=jax.ShapeDtypeStruct(sensitivity.shape,...  37 us
    unnamed x1, local copies, waits for them, and re-layouts  0.8 us

profile of v8, /device:TPU:1, one launch (start us, length us, event | category | flops | bytes accessed | tf_op | source)
XLA Modules:
  0.0 37.9 jit_solution(6915121584114956302)
XLA Ops:
  0.0 37.0 %update.1 = f32[4,64,512]{2,1,0:T(8,128)S(1)} custom-call(f32[4,512,512]{2,1,0:T(8,128)} %image_hbm.1, f32[4,64,512]{2,1,0:T(8,128)} %sens_hbm.1, bf16[2,512,512]{2,1,0:T(8,128)(2,1)} %rx_hbm.1, bf16[2,512,512]{2,1,0:T(8,128)(2,1)} %ry_hbm.1, bf16[2,16,512]{2,1,0:T(8,128)(2,1)} %tof_hbm.1, f32[2,128,128]{2,1,0:T(8,128)} %mix_hbm.1, f32[512,128]{1,0:T(8,128)} %bitcast.2, ...), custom_call_target="tpu_custom_call" | custom-call | tf_op jit(solution)/shard_map/update/pallas_call | solution.py:345
  37.1 0.8 %copy.10 = f32[4,64,512]{2,1,0:T(8,128)} copy(f32[4,64,512]{2,1,0:T(8,128)S(1)} %update.1) | data formatting | bytes 1048576

commit v9 on v8

--- a/solution.py
+++ b/solution.py
@@ -98,6 +98,9 @@
             for n, (a, b) in enumerate(pieces)
         ]
 
+    for o in range(1, chips):
+        for v in range(views):
+            ry[o, v] = jnp.zeros(ry.shape[2:], BF16)
     part = lax.broadcasted_iota(jnp.int32, (PIECE, width), 1) // PIECE
     keep = [jnp.where(part == g, 1.0, 0.0).astype(BF16) for g in range(width // PIECE)]
 
@@ -173,14 +176,6 @@
             if v == 0 and z == 0:
                 for copy in loads[:4]:
                     copy.wait()
-                tall = [tof_ref[u].astype(F32) for u in range(views) for n in range(own)]
-                tof_tall[inner, :] = jnp.concatenate(tall, axis=0).T.astype(BF16)
-                for copy in mine_near:
-                    copy.start()
-                for b in range(chips):
-                    for u in range(views):
-                        rx_pack[b, u] = pack(rx.at[u], b)
-                        ry_pack[b, u] = pack(ry.at[0, u], b)
             elif v == 0:
                 loads[3 + z].wait()
             low = image[z].astype(BF16)
@@ -197,6 +192,14 @@
             pl.semaphore_wait(barrier, parts - 1 + len(peers))
         send(v)
         if v == 0:
+            tall = [tof_ref[u].astype(F32) for u in range(views) for n in range(own)]
+            tof_tall[inner, :] = jnp.concatenate(tall, axis=0).T.astype(BF16)
+            for copy in mine_near:
+                copy.start()
+            for b in range(chips):
+                for u in range(views):
+                    rx_pack[b, u] = pack(rx.at[u], b)
+                    ry_pack[b, u] = pack(ry.at[0, u], b)
             for o in (1, 3, 2):
                 for copy in bands(o):
                     copy.start()
@@ -256,9 +259,6 @@
                 staged[pl.ds(n * own + g, parts, stride=rank), :] = held[g]
         back[v] = staged[...].reshape(parts, rank, lanes).astype(BF16)
         send_back(v)
-    for o in range(1, chips):
-        for v in range(views):
-            ry[o, v] = jnp.zeros(ry.shape[2:], BF16)
     for o in (1, 3, 2):
         for copy in bands(o):
             copy.wait_recv()

time: 37.9 us -> 38 us (level)
  no operation moved by 1% of the time
where the time goes in v9:
time: 38 us; the launch traced here: 37.9 us
  Pallas kernels  37.1 us (98%)
  local copies, waits for them, and re-layouts  0.8 us (2%)
    pallas_call x1, Pallas kernels, local(): pl.pallas_call(kernel, out_shape=jax.ShapeDtypeStruct(sensitivity.shape,...  37.1 us
    unnamed x1, local copies, waits for them, and re-layouts  0.8 us

profile of v9, /device:TPU:1, one launch (start us, length us, event | category | flops | bytes accessed | tf_op | source)
XLA Modules:
  0.0 37.9 jit_solution(16031249603163206881)
XLA Ops:
  0.0 37.1 %update.1 = f32[4,64,512]{2,1,0:T(8,128)S(1)} custom-call(f32[4,512,512]{2,1,0:T(8,128)} %image_hbm.1, f32[4,64,512]{2,1,0:T(8,128)} %sens_hbm.1, bf16[2,512,512]{2,1,0:T(8,128)(2,1)} %rx_hbm.1, bf16[2,512,512]{2,1,0:T(8,128)(2,1)} %ry_hbm.1, bf16[2,16,512]{2,1,0:T(8,128)(2,1)} %tof_hbm.1, f32[2,128,128]{2,1,0:T(8,128)} %mix_hbm.1, f32[512,128]{1,0:T(8,128)} %bitcast.2, ...), custom_call_target="tpu_custom_call" | custom-call | tf_op jit(solution)/shard_map/update/pallas_call | solution.py:345
  37.1 0.8 %copy.10 = f32[4,64,512]{2,1,0:T(8,128)} copy(f32[4,64,512]{2,1,0:T(8,128)S(1)} %update.1) | data formatting | bytes 1048576
